TPU v7x, 128 devices: a whole 4x4x4 slice. The times are simulated.
128 devices in a mesh: grp: 4 (over y), fsdp: 32 (over x, z, core).
Axes of the slice: x: 4, y: 4, z: 4, core: 2. Of those that a mesh axis runs over, the one named last changes fastest.
Arguments:
- hidden: bfloat16 [256, 257, 1024], P(('grp', 'fsdp')), may hold values from -6 to 6
- ln1_gain: float32 [1024], replicated, may hold values from 0.25 to 1.75
- w_qkv: bfloat16 [1024, 3072], P('fsdp'), may hold values from -0.1875 to 0.1875
- w_out: bfloat16 [1024, 1024], P('fsdp'), may hold values from -0.1875 to 0.1875
- ln2_gain: float32 [1024], replicated, may hold values from 0.25 to 1.75
- w_up: bfloat16 [1024, 4096], P('fsdp'), may hold values from -0.1875 to 0.1875
- w_down: bfloat16 [4096, 1024], P('fsdp'), may hold values from -0.09375 to 0.09375
- post_gain: float32 [1024], replicated, may hold values from 0.25 to 1.75
- w_proj: bfloat16 [1024, 256], replicated, may hold values from -0.1875 to 0.1875
- table: float32 [128, 2048, 256], P(('grp', 'fsdp')), may hold values from -6 to 6
- accum: float32 [128, 2048, 256], P(('grp', 'fsdp')), may hold values from 0.1 to 4
- place: int32 [128], replicated, may hold values from 0 to 127, each once
- lookup_table: int32 [16384, 1], P(('grp', 'fsdp')), may hold values from 0 to 127; in each aligned block of 128 rows (0 to 127, 128 to 255, ...) at most 2 rows name the same one
- lookup_row: int32 [16384], P(('grp', 'fsdp')), may hold values from 0 to 2047
Outputs:
- table_new: float32 [128, 2048, 256], P(('grp', 'fsdp'))
- accum_new: float32 [128, 2048, 256], P(('grp', 'fsdp'))
- content_grad: float32 [256, 256], P(('grp', 'fsdp'))
- proj_grad: float32 [1024, 256], P(('grp', 'fsdp'))
Inputs may be any that keep to these rules, and one draw needn't show every extreme that they name: `lookup_table`: within the lookups of one device (aligned blocks of 128), no table is named more than 2 times, a bound that some block reaches. `place`: every device holds exactly one table.
All inputs are finite; a program needn't handle non-finite values.
Results may differ from a plain program's by a relative error of at most 0.0044.
Values may be sent and summed in bfloat16 or wider, within the bound.
A program may use at most 192 MiB of HBM per device.

v0:
```python
import math

import jax
import jax.numpy as jnp
from jax import lax
from jax.sharding import Mesh
from jax.sharding import PartitionSpec as P

HEADS = 16
LOOK_IMG = 64
FSDP = ("fsdp_0", "fsdp_1", "fsdp_2")
GRP_FSDP = ("grp", "fsdp_0", "fsdp_1", "fsdp_2")


epsilon = 1e-06
learn_rate = 0.5


def sent_together(arrays, axis, dim, along):
    widths = [a.shape[along] for a in arrays]
    both = jnp.concatenate(arrays, axis=along)
    out = lax.all_gather(both, axis, axis=dim, tiled=True)
    return tuple(jnp.split(out, [sum(widths[:k]) for k in range(1, len(widths))], axis=along))


def in_blocks(array, dim, devices):
    shape = array.shape
    tiles = array.reshape(*shape[:dim], devices, shape[dim] // devices, *shape[dim + 1 :])
    return jnp.moveaxis(tiles, dim, 0)


def laid_out(tiles, dim):
    tiles = jnp.moveaxis(tiles, 0, dim)
    shape = tiles.shape
    return tiles.reshape(*shape[:dim], shape[dim] * shape[dim + 1], *shape[dim + 2 :])


def turned_blocks(tiles, axes, sequence):
    shape = [lax.axis_size(a) for a in axes]
    tiles = tiles.reshape(*shape, *tiles.shape[1:])
    for k in sequence:
        tiles = lax.all_to_all(tiles, axes[k], split_axis=k, concat_axis=k, tiled=True)
    return tiles.reshape(-1, *tiles.shape[len(axes) :])


def core_and_chips(array, groups, sequence, split_dim, concat_dim):
    devices = lax.axis_size(groups[0]) * lax.axis_size(groups[1])
    tiles = in_blocks(array, split_dim, devices)
    return laid_out(turned_blocks(tiles, groups, sequence), concat_dim)


def layer_norm(values, gain):
    center = jnp.mean(values, axis=-1, keepdims=True)
    shifted = values - center
    spread = jnp.mean(shifted * shifted, axis=-1, keepdims=True)
    return shifted * lax.rsqrt(spread + epsilon) * gain


def attend(qkv, images, seq, width):
    head_dim = width // HEADS
    parts = qkv.reshape(images, seq, 3, HEADS, head_dim)
    scores = jnp.einsum(
        "bqhd,bkhd->bhqk", parts[:, :, 0], parts[:, :, 1], preferred_element_type=jnp.float32
    ) / math.sqrt(head_dim)
    probs = jax.nn.softmax(scores, axis=-1).astype(jnp.bfloat16)
    mixed = jnp.einsum("bhqk,bkhd->bqhd", probs, parts[:, :, 2], preferred_element_type=jnp.float32)
    return mixed.astype(jnp.bfloat16).reshape(images * seq, width)


def on_device(
    hidden,
    ln1_gain,
    w_qkv,
    w_out,
    ln2_gain,
    w_up,
    w_down,
    post_gain,
    w_proj,
    table,
    accum,
    place,
    lookup_table,
    lookup_row,
):
    images, seq, width = hidden.shape
    count = images * seq
    tokens = hidden.reshape(count, width)
    full_qkv, full_out, full_up, full_down = (
        *sent_together((w_qkv, w_out, w_up), FSDP, 0, 1),
        lax.all_gather(w_down, FSDP, axis=0, tiled=True),
    )
    normed = layer_norm(tokens.astype(jnp.float32), ln1_gain).astype(jnp.bfloat16)
    qkv = jnp.dot(normed, full_qkv, preferred_element_type=jnp.float32)
    mixed = attend(qkv.astype(jnp.bfloat16), images, seq, width)
    projected = jnp.dot(mixed, full_out, preferred_element_type=jnp.float32)
    resid = (tokens.astype(jnp.float32) + projected).astype(jnp.bfloat16)
    normed_two = layer_norm(resid.astype(jnp.float32), ln2_gain).astype(jnp.bfloat16)
    upward = jnp.dot(normed_two, full_up, preferred_element_type=jnp.float32)
    active = jax.nn.gelu(upward, approximate=False).astype(jnp.bfloat16)
    downward = jnp.dot(active, full_down, preferred_element_type=jnp.float32)
    final = resid.astype(jnp.float32) + downward
    posted = layer_norm(final, post_gain).reshape(images, seq, width)
    pooled = jnp.mean(posted, axis=1).astype(jnp.bfloat16)
    content = jnp.dot(pooled, w_proj, preferred_element_type=jnp.float32)
    scale = lax.rsqrt(jnp.mean(content * content, axis=-1, keepdims=True) + epsilon)
    unit = content * scale
    proj_width = unit.shape[1]
    local_table = table[0]
    n_devices = lax.axis_size(GRP_FSDP)
    tables_count = place.shape[0]
    table_ids = jnp.arange(tables_count, dtype=jnp.int32)
    look_dev = lookup_row.shape[0]
    slots = max(2, (2 * look_dev + n_devices - 1) // n_devices)
    owners = jnp.sum(jnp.where(lookup_table == table_ids[None, :], place[None, :], 0), axis=1)
    hits = (owners[:, None] == jnp.arange(n_devices, dtype=jnp.int32)[None, :]).astype(jnp.int32)
    earlier = jnp.cumsum(hits, axis=0) - hits
    position = jnp.sum(earlier * hits, axis=1)
    target = owners * slots + position
    spread_unit = jnp.repeat(unit, LOOK_IMG, axis=0)
    send_vec = jnp.zeros((n_devices * slots, proj_width), jnp.float32).at[target].set(spread_unit)
    send_rows = jnp.full((n_devices * slots,), -1, jnp.int32).at[target].set(lookup_row)
    got_vec, got_rows = (
        core_and_chips(
            send_vec.reshape(n_devices, slots, proj_width),
            (("grp", "fsdp_0", "fsdp_1"), "fsdp_2"),
            (1, 0),
            0,
            0,
        ),
        core_and_chips(
            send_rows.reshape(n_devices, slots),
            (("grp", "fsdp_0", "fsdp_1"), "fsdp_2"),
            (1, 0),
            0,
            0,
        ),
    )
    flat_rows = got_rows.reshape(-1)
    valid = flat_rows >= 0
    safe_rows = jnp.where(valid, flat_rows, 0)
    diff = jnp.where(valid[:, None], local_table[safe_rows] - got_vec.reshape(-1, proj_width), 0.0)
    grad_rows = jnp.zeros(local_table.shape, jnp.float32).at[safe_rows].add(diff)
    returned = lax.all_to_all(
        -diff.reshape(n_devices, slots, proj_width),
        GRP_FSDP,
        split_axis=0,
        concat_axis=0,
        tiled=True,
    )
    per_lookup = returned.reshape(-1, proj_width)[target]
    grad_unit = jnp.sum(per_lookup.reshape(images, LOOK_IMG, proj_width), axis=1)
    accum_new = accum[0] + grad_rows * grad_rows
    table_new = local_table - learn_rate * grad_rows / jnp.sqrt(accum_new)
    inner = jnp.mean(grad_unit * unit, axis=-1, keepdims=True)
    content_grad = scale * (grad_unit - unit * inner)
    share = width // n_devices
    every_grad = lax.all_gather(content_grad, GRP_FSDP, axis=0, tiled=True)
    my_columns = lax.all_to_all(
        pooled.reshape(images, n_devices, share), GRP_FSDP, split_axis=1, concat_axis=0, tiled=True
    )
    column_block = my_columns.reshape(-1, share).astype(jnp.float32)
    proj_grad = jnp.dot(
        column_block.T,
        every_grad,
        precision=lax.Precision.HIGHEST,
        preferred_element_type=jnp.float32,
    )
    return (table_new[None], accum_new[None], content_grad, proj_grad)


def solution(mesh):
    torus = Mesh(
        mesh.devices.reshape(mesh.shape["grp"], 4, 4, 2), ("grp", "fsdp_0", "fsdp_1", "fsdp_2")
    )
    in_specs = (
        P(GRP_FSDP, None, None),
        P(),
        P(FSDP, None),
        P(FSDP, None),
        P(),
        P(FSDP, None),
        P(FSDP, None),
        P(),
        P(),
        P(GRP_FSDP, None, None),
        P(GRP_FSDP, None, None),
        P(),
        P(GRP_FSDP, None),
        P(GRP_FSDP),
    )
    out_specs = (
        P(GRP_FSDP, None, None),
        P(GRP_FSDP, None, None),
        P(GRP_FSDP, None),
        P(GRP_FSDP, None),
    )
    return jax.shard_map(
        on_device, mesh=torus, in_specs=in_specs, out_specs=out_specs, check_vma=False
    )
```

profile of v0, /device:TPU:1, one launch (start us, length us, event | category | flops | bytes accessed | tf_op | source)
XLA Modules:
  0.0 299.0 jit_solution(8550466060743165538)
XLA Ops:
  7.2 1.9 pad_maximum_fusion
  9.2 0.7 all-gather.6.cloned.1.call-update
  9.9 0.8 select_reduce_fusion.1
  10.9 0.2 reduce_window_sum.11
  11.0 0.2 select_reduce_fusion
  11.2 1.1 scatter_custom_fusion
  12.3 0.2 reshape_reshape_reshape.14
  12.7 4.7 %all_to_all.40 = s32[2,1,128]{2,1,0:T(1,128)S(1)} all-to-all(s32[2,1,128]{2,1,0:T(1,128)S(1)} %reshape.241), channel_id=1, replica_groups=mesh['grp'=4,'fsdp_0'=4,'fsdp_1'=4,'fsdp_2'=2] {'fsdp_2'}, dimensions={0} | all-to-all | bytes 2048 | tf_op jit(solution)/shard_map/all_to_all | solution.py:42
  17.4 0.5 broadcast.233
  17.9 0.7 reduce.2
  18.7 0.7 copy.51
  19.4 11.8 %all-to-all-start.1 = ((s32[64,2,1,2]{3,1,2,0:T(2,128)}), s32[64,2,1,2]{3,1,2,0:T(2,128)S(1)}, u32[]{:S(2)}, u32[]{:S(2)}) async-start(s32[64,2,1,2]{3,1,2,0:T(2,128)} %copy.51), calls=%async_computation.1 | async-start | bytes 131072 | tf_op jit(solution)/shard_map/all_to_all | solution.py:42
  31.2 2.1 convert_reduce_fusion.1
  33.4 2.8 multiply_reduce_fusion.2
  36.2 1.6 copy.52
  37.8 0.1 copy.74
  37.9 1.5 reshape.190
  39.6 0.6 all-to-all-done.1
  40.3 0.1 ge.24
  40.5 0.2 reshape_reshape_reshape.15
  40.6 47.2 %all-gather.4.cloned.1.call-done = bf16[1024,8192]{1,0:T(8,128)(2,1)} async-done(((bf16[32,8192]{1,0:T(8,128)(2,1)}), bf16[1024,8192]{1,0:T(8,128)(2,1)}) %all-gather.4.cloned.1.call-update) | async-done | bytes 16777232 | tf_op jit(solution)/shard_map/all_gather | solution.py:22
  87.9 8.8 %fusion.20 = bf16[514,3072]{1,0:T(8,128)(2,1)} fusion(bf16[1024,8192]{1,0:T(8,128)(2,1)} %all-gather.4.cloned.1.call-done, f32[514,1024]{1,0:T(8,128)} %reshape.190, f32[1024]{0:T(1024)S(1)} %copy-done.5, f32[514]{0:T(1024)S(1)} %rsqrt.37, f32[514]{0:T(1024)S(1)} %div.50), kind=kOutput, calls=%fused_computation.35 | convolution fusion | flops 3237492736 | bytes 11587600 | tf_op jit(solution)/shard_map/dot_general | solution.py:94
  96.6 8.7 %reshape.234 = bf16[2,257,3,16,64]{4,3,2,1,0:T(8,128)(2,1)} reshape(bf16[514,3072]{1,0:T(8,128)(2,1)} %fusion.20) | data formatting | bytes 6316032 | tf_op jit(solution)/shard_map/reshape | solution.py:61
  105.4 6.1 %fusion.107 = (bf16[2,257,1,16,64]{4,3,2,1,0:T(8,128)(2,1)S(1)}, bf16[2,257,1,16,64]{4,3,2,1,0:T(8,128)(2,1)}, bf16[2,257,1,16,64]{4,3,2,1,0:T(8,128)(2,1)}) fusion(bf16[2,257,3,16,64]{4,3,2,1,0:T(8,128)(2,1)} %reshape.234), kind=kLoop, calls=%fused_computation.139 | loop fusion | bytes 6316032 | tf_op jit(solution)/shard_map/slice | solution.py:66
  111.4 4.3 %copy.72 = bf16[2,257,1,16,64]{1,4,3,0,2:T(8,128)(2,1)} copy(bf16[2,257,1,16,64]{4,3,2,1,0:T(8,128)(2,1)} %get-tuple-element.5) | data formatting | bytes 2105344
  115.7 4.3 %copy.73 = bf16[2,257,1,16,64]{1,4,3,0,2:T(8,128)(2,1)} copy(bf16[2,257,1,16,64]{4,3,2,1,0:T(8,128)(2,1)} %get-tuple-element.6) | data formatting | bytes 2105344
  120.0 3.8 %copy.71 = bf16[2,257,1,16,64]{1,4,3,0,2:T(8,128)(2,1)} copy(bf16[2,257,1,16,64]{4,3,2,1,0:T(8,128)(2,1)S(1)} %get-tuple-element.4) | data formatting | bytes 2105344
  123.8 9.2 %fusion.41 = f32[2,16,257,257]{2,3,1,0:T(8,128)} fusion(bf16[2,257,1,16,64]{1,4,3,0,2:T(8,128)(2,1)} %copy.73, bf16[2,257,1,16,64]{1,4,3,0,2:T(8,128)(2,1)} %copy.72), kind=kOutput, calls=%fused_computation.55 | convolution fusion | flops 270536704 | bytes 10559616 | tf_op jit(solution)/shard_map/bqhd,bkhd->bhqk/dot_general | solution.py:62
  133.0 17.3 %fusion.108 = (f32[2,16,257]{2,1,0:T(8,128)S(1)}, f32[2,16,257,257]{2,3,1,0:T(8,128)}) fusion(f32[2,16,257,257]{2,3,1,0:T(8,128)} %fusion.41), kind=kOutput, calls=%fused_computation.140 | output fusion | flops 8454528 | bytes 16941440 | tf_op jit(solution)/shard_map/sub | solution.py:65
  150.3 6.4 %fusion.45 = bf16[2,257,16,64]{1,3,2,0:T(8,128)(2,1)S(1)} fusion(f32[2,16,257,257]{2,3,1,0:T(8,128)} %get-tuple-element.10, f32[2,16,257]{2,1,0:T(8,128)S(1)} %get-tuple-element.9, bf16[2,257,1,16,64]{1,4,3,0,2:T(8,128)(2,1)S(1)} %copy-done.2), kind=kOutput, calls=%fused_computation.59 | convolution fusion | flops 275290176 | bytes 10592512 | tf_op jit(solution)/shard_map/bhqk,bkhd->bqhd/dot_general | solution.py:66
  156.7 1.6 copy.61
  158.4 1.2 reshape.184
  159.6 3.7 %convert_reduce_fusion = (f32[514]{0:T(1024)S(1)}, bf16[514,1024]{1,0:T(8,128)(2,1)S(1)}) fusion(f32[514,1024]{1,0:T(8,128)} %reshape.190, bf16[514,1024]{0,1:T(8,128)(2,1)S(1)} %reshape.184, bf16[1024,8192]{1,0:T(8,128)(2,1)} %all-gather.4.cloned.1.call-done), kind=kOutput, calls=%fused_computation.39 | convolution fusion | flops 1080040960 | bytes 6334472 | tf_op jit(solution)/shard_map/dot_general | solution.py:96
  163.3 0.4 fusion.31
  163.7 26.2 %fusion.40.clone.4 = bf16[514,4096]{1,0:T(8,128)(2,1)} fusion(bf16[1024,8192]{1,0:T(8,128)(2,1)} %all-gather.4.cloned.1.call-done, bf16[514,1024]{1,0:T(8,128)(2,1)S(1)} %get-tuple-element.12, f32[1024]{0:T(1024)S(1)} %copy-done.6, f32[514]{0:T(1024)S(1)} %add_rsqrt_fusion.2, f32[514]{0:T(1024)S(1)} %broadcast_multiply_fusion.2), kind=kOutput, calls=%fused_computation.13.clone.clone.clone.clone.clone.clone.1 | convolution fusion | flops 4451223552 | bytes 13660176 | tf_op jit(solution)/shard_map/dot_general | solution.py:99
  190.0 8.7 %fusion.109 = (f32[514]{0:T(1024)S(1)}, f32[514,1024]{1,0:T(8,128)S(1)}) fusion(bf16[4096,1024]{1,0:T(8,128)(2,1)} %all-gather.6.cloned.1.call-done, bf16[514,1024]{1,0:T(8,128)(2,1)S(1)} %get-tuple-element.12, bf16[514,4096]{1,0:T(8,128)(2,1)} %fusion.40.clone.4), kind=kOutput, calls=%fused_computation.141 | convolution fusion | flops 4313323008 | bytes 15759368 | tf_op jit(solution)/shard_map/dot_general | solution.py:101
  198.7 0.4 multiply_reduce_fusion.1
  199.1 1.7 multiply_multiply_fusion.5
  200.8 1.8 reshape.185
  202.6 0.1 reduce_sum.126
  202.8 0.3 multiply_reduce_fusion.4
  203.2 1.1 scatter_custom_fusion.1
  204.2 0.1 reshape_reshape_reshape.16
  204.5 4.0 %all_to_all.41 = f32[64,2,1,2,256]{4,3,0,2,1:T(2,128)S(1)} all-to-all(f32[64,2,1,2,256]{4,3,0,2,1:T(2,128)S(1)} %copy.62), channel_id=1, replica_groups=mesh['grp'=4,'fsdp_0'=4,'fsdp_1'=4,'fsdp_2'=2] {'fsdp_2'}, dimensions={1} | all-to-all | bytes 524288 | tf_op jit(solution)/shard_map/all_to_all | solution.py:42
  208.5 0.7 copy.63
  209.2 8.1 %all-to-all-start.3 = ((f32[64,2,1,2,256]{4,3,1,2,0:T(2,128)}), f32[64,2,1,2,256]{4,3,1,2,0:T(2,128)S(1)}, u32[]{:S(2)}, u32[]{:S(2)}) async-start(f32[64,2,1,2,256]{4,3,1,2,0:T(2,128)} %copy.63), calls=%async_computation.3 | async-start | bytes 524288 | tf_op jit(solution)/shard_map/all_to_all | solution.py:42
  217.4 2.6 gather_fusion
  219.9 0.1 gather.9
  220.1 0.1 convert_element_type.64
  220.2 0.7 copy.66
  220.9 6.4 %all-to-all-done.3 = f32[64,2,1,2,256]{4,3,1,2,0:T(2,128)S(1)} async-done(((f32[64,2,1,2,256]{4,3,1,2,0:T(2,128)}), f32[64,2,1,2,256]{4,3,1,2,0:T(2,128)S(1)}, u32[]{:S(2)}, u32[]{:S(2)}) %all-to-all-start.3) | async-done | bytes 262176 | tf_op jit(solution)/shard_map/all_to_all | solution.py:42
  227.2 1.0 fusion.65
  228.2 5.1 %all-to-all-start.4 = ((f32[128,2,256]{2,1,0:T(2,128)}), f32[128,2,256]{2,1,0:T(2,128)S(1)}, u32[]{:S(2)}, u32[]{:S(2)}) async-start(f32[128,2,256]{2,1,0:T(2,128)} %fusion.65), calls=%async_computation.4 | async-start | bytes 524288 | tf_op jit(solution)/shard_map/all_to_all | solution.py:144
  233.3 0.9 reshape_reshape_reshape.17
  234.2 3.9 %scatter_custom_fusion.2 = f32[2048,256]{1,0:T(8,128)} fusion(s32[256]{0:T(256)S(1)} %bitcast.73, f32[]{:T(128)} %constant.41.clone.1, f32[256,256]{1,0:T(8,128)S(1)} %gather_fusion, f32[256,256]{1,0:T(8,128)} %reshape_reshape_reshape.17, pred[256]{0:T(512)(128)(4,1)S(1)} %ge.24), kind=kCustom, calls=%fused_computation.67 | custom fusion | flops 196608 | bytes 2622976 | tf_op jit(solution)/shard_map/scatter-add | solution.py:143
  238.0 4.7 %fusion.63 = (f32[1,2048,256]{2,1,0:T(8,128)}, f32[1,2048,256]{2,1,0:T(8,128)}) fusion(f32[2048,256]{1,0:T(8,128)} %scatter_custom_fusion.2, f32[1,2048,256]{2,1,0:T(8,128)} %param.24, f32[1,2048,256]{2,1,0:T(8,128)S(1)} %copy-done.1), kind=kLoop, calls=%fused_computation.69 | loop fusion | flops 2621440 | bytes 10485760 | tf_op jit(solution)/shard_map/broadcast_in_dim | solution.py:169
  242.7 1.5 all-to-all-done.4
  244.2 8.3 %all-to-all-start.5 = ((bf16[2,128,8]{2,0,1:T(2,128)(2,1)}), bf16[2,128,8]{2,0,1:T(2,128)(2,1)S(1)}, u32[]{:S(2)}, u32[]{:S(2)}) async-start(bf16[2,128,8]{2,0,1:T(2,128)(2,1)} %copy.66), calls=%async_computation.5 | async-start | bytes 131072 | tf_op jit(solution)/shard_map/all_to_all | solution.py:159
  252.6 0.2 reshape.187
  252.8 0.8 gather_fusion.1
  253.6 0.2 multiply_reduce_fusion.3
  253.8 37.0 %all-gather = f32[128,2,256]{2,1,0:T(2,128)S(1)} all-gather(f32[1,2,256]{2,1,0:T(2,128)S(1)} %bitcast.69), channel_id=1, replica_groups=mesh['grp'=4,'fsdp_0'=4,'fsdp_1'=4,'fsdp_2'=2] {'grp','fsdp_0','fsdp_1',..., dimensions={0}, use_global_device_ids=true | all-gather | bytes 264192 | tf_op jit(solution)/shard_map/all_gather | solution.py:158
  290.9 0.2 reshape.232
  291.0 0.8 fusion.114
  (46 shorter events, 1.2 us)
Async XLA Ops:
  7.2 195.6 %copy-start = (bf16[1024,256]{1,0:T(8,128)(2,1)S(1)}, bf16[1024,256]{1,0:T(8,128)(2,1)}, u32[]{:S(2)}) copy-start(bf16[1024,256]{1,0:T(8,128)(2,1)} %param.22) | copy-start | bytes 1572868
  7.2 80.7 %all-gather.4.cloned.1.call-start = ((), (), s32[]{:S(2)}) async-start(), calls=%async_computation.6 | async-start | bytes 17301504 | tf_op jit(solution)/shard_map/all_gather | solution.py:22
  9.1 78.7 %copy-start.5 = (f32[1024]{0:T(1024)S(1)}, f32[1024]{0:T(1024)}, u32[]{:S(2)}) copy-start(f32[1024]{0:T(1024)} %param.15) | copy-start | bytes 12292
  9.2 180.8 %all-gather.6.cloned.1.call-start = ((), (), s32[]{:S(2)}) async-start(), calls=%async_computation.7 | async-start | bytes 8650752 | tf_op jit(solution)/shard_map/all_gather | solution.py:91
  19.4 20.8 %all-to-all-start.1 = ((s32[64,2,1,2]{3,1,2,0:T(2,128)}), s32[64,2,1,2]{3,1,2,0:T(2,128)S(1)}, u32[]{:S(2)}, u32[]{:S(2)}) async-start(s32[64,2,1,2]{3,1,2,0:T(2,128)} %copy.51), calls=%async_computation.1 | async-start | bytes 131072 | tf_op jit(solution)/shard_map/all_to_all | solution.py:42
  133.0 17.3 %copy-start.2 = (bf16[2,257,1,16,64]{1,4,3,0,2:T(8,128)(2,1)S(1)}, bf16[2,257,1,16,64]{1,4,3,0,2:T(8,128)(2,1)}, u32[]{:S(2)}) copy-start(bf16[2,257,1,16,64]{1,4,3,0,2:T(8,128)(2,1)} %copy.71) | copy-start | bytes 3158020
  159.6 4.1 %copy-start.6 = (f32[1024]{0:T(1024)S(1)}, f32[1024]{0:T(1024)}, u32[]{:S(2)}) copy-start(f32[1024]{0:T(1024)} %param.18) | copy-start | bytes 12292
  190.0 9.1 %copy-start.4 = (f32[1024]{0:T(1024)S(1)}, f32[1024]{0:T(1024)}, u32[]{:S(2)}) copy-start(f32[1024]{0:T(1024)} %param.21) | copy-start | bytes 12292
  202.7 35.3 %copy-start.1 = (f32[1,2048,256]{2,1,0:T(8,128)S(1)}, f32[1,2048,256]{2,1,0:T(8,128)}, u32[]{:S(2)}) copy-start(f32[1,2048,256]{2,1,0:T(8,128)} %param.23) | copy-start | bytes 6291460
  209.2 18.0 %all-to-all-start.3 = ((f32[64,2,1,2,256]{4,3,1,2,0:T(2,128)}), f32[64,2,1,2,256]{4,3,1,2,0:T(2,128)S(1)}, u32[]{:S(2)}, u32[]{:S(2)}) async-start(f32[64,2,1,2,256]{4,3,1,2,0:T(2,128)} %copy.63), calls=%async_computation.3 | async-start | bytes 524288 | tf_op jit(solution)/shard_map/all_to_all | solution.py:42
  228.2 16.0 %all-to-all-start.4 = ((f32[128,2,256]{2,1,0:T(2,128)}), f32[128,2,256]{2,1,0:T(2,128)S(1)}, u32[]{:S(2)}, u32[]{:S(2)}) async-start(f32[128,2,256]{2,1,0:T(2,128)} %fusion.65), calls=%async_computation.4 | async-start | bytes 524288 | tf_op jit(solution)/shard_map/all_to_all | solution.py:144
  244.2 46.8 %all-to-all-start.5 = ((bf16[2,128,8]{2,0,1:T(2,128)(2,1)}), bf16[2,128,8]{2,0,1:T(2,128)(2,1)S(1)}, u32[]{:S(2)}, u32[]{:S(2)}) async-start(bf16[2,128,8]{2,0,1:T(2,128)(2,1)} %copy.66), calls=%async_computation.5 | async-start | bytes 131072 | tf_op jit(solution)/shard_map/all_to_all | solution.py:159
  253.8 38.0 %copy-start.3 = (f32[2,256]{1,0:T(2,128)}, f32[2,256]{1,0:T(2,128)S(1)}, u32[]{:S(2)}) copy-start(f32[2,256]{1,0:T(2,128)S(1)} %subtract_multiply_fusion) | copy-start | bytes 6148
Sparse Core Ops, SparseCore 0:
  10.8 76.9 all-gather.3
  90.1 52.2 all-gather.5
where the time goes:
time: 302 us; the launch traced here: 299 us
  matrix products  64.1 us (21%)
  waiting for transfers between devices  56.4 us (19%)
  local copies, waits for them, and re-layouts  46 us (15%)
  blocking collectives  45.8 us (15%)
  other arithmetic  38.7 us (13%)
  starting transfers between devices  33.3 us (11%)
  between operations  14.7 us (5%)
    all_gather x1, waiting for transfers between devices, sent_together(): out = lax.all_gather(both, axis, axis=dim, tiled=True)  47.2 us
    all_gather x1, blocking collectives, on_device(): every_grad = lax.all_gather(content_grad, GRP_FSDP, axis=0, tiled=True)  37 us
    dot_general x1, matrix products, on_device(): upward = jnp.dot(normed_two, full_up, preferred_element_type=jnp.float32)  26.2 us
    all_to_all x2, starting transfers between devices, turned_blocks(): lax.all_to_all(tiles, axes[k], split_axis=k, concat_axis=k, tiled=True)  19.8 us
    sub x1, other arithmetic, attend(): probs = jax.nn.softmax(scores, axis=-1).astype(jnp.bfloat16)  17.3 us
    unnamed x22, local copies, waits for them, and re-layouts  13 us
    dot_general x1, matrix products, attend(): jnp.einsum('bqhd,bkhd->bhqk', parts[:, :, 0], parts[:, :, 1], preferred_e...  9.2 us
    dot_general x1, matrix products, on_device(): qkv = jnp.dot(normed, full_qkv, preferred_element_type=jnp.float32)  8.78 us
  transfers between devices with their start and end apart: 6, of which 4 were waited for; matrix products, arithmetic and copies ran while one was open for 43% of the time, Pallas kernels for 0%

commit v1 on v0

--- a/solution.py
+++ b/solution.py
@@ -67,6 +67,24 @@
     return mixed.astype(jnp.bfloat16).reshape(images * seq, width)
 
 
+def named_counts(lookup_table, lookup_row, place, images, rows_dev, me):
+    table_ids = jnp.arange(place.shape[0], dtype=jnp.int32)
+    owners = jnp.sum(jnp.where(lookup_table == table_ids[None, :], place[None, :], 0), axis=1)
+    image = jnp.arange(lookup_row.shape[0], dtype=jnp.int32) // LOOK_IMG
+    named = (owners * rows_dev + lookup_row) * images + image
+    every = lax.all_gather(named[None, :], GRP_FSDP, axis=0, tiled=True)
+    code = every - me * (rows_dev * images)
+    mine = (code >= 0) & (code < rows_dev * images)
+    first = jnp.max(jnp.where(mine, code, -1), axis=1)
+    second = jnp.min(jnp.where(mine, code, rows_dev * images), axis=1)
+    second = jnp.where(jnp.sum(mine.astype(jnp.int32), axis=1) > 1, second, -1)
+    wanted = jnp.arange(rows_dev, dtype=jnp.int32)[:, None] * images + (
+        jnp.arange(every.shape[0] * images, dtype=jnp.int32) % images
+    )[None, :]
+    hit = lambda codes: (wanted == jnp.repeat(codes, images)[None, :]).astype(jnp.float32)
+    return hit(first) + hit(second)
+
+
 def on_device(
     hidden,
     ln1_gain,
@@ -86,6 +104,15 @@
     images, seq, width = hidden.shape
     count = images * seq
     tokens = hidden.reshape(count, width)
+    n_devices = lax.axis_size(GRP_FSDP)
+    me = lax.axis_index(GRP_FSDP)
+    local_table = table[0]
+    rows_dev = local_table.shape[0]
+    counts = named_counts(lookup_table, lookup_row, place, images, rows_dev, me)
+    row_sums = lax.psum(
+        lax.dot_general(counts, local_table, (((0,), (0,)), ((), ())), precision=lax.Precision.HIGHEST, preferred_element_type=jnp.float32),
+        GRP_FSDP,
+    )
     full_qkv, full_out, full_up, full_down = (
         *sent_together((w_qkv, w_out, w_up), FSDP, 0, 1),
         lax.all_gather(w_down, FSDP, axis=0, tiled=True),
@@ -105,67 +132,23 @@
     content = jnp.dot(pooled, w_proj, preferred_element_type=jnp.float32)
     scale = lax.rsqrt(jnp.mean(content * content, axis=-1, keepdims=True) + epsilon)
     unit = content * scale
-    proj_width = unit.shape[1]
-    local_table = table[0]
-    n_devices = lax.axis_size(GRP_FSDP)
-    tables_count = place.shape[0]
-    table_ids = jnp.arange(tables_count, dtype=jnp.int32)
-    look_dev = lookup_row.shape[0]
-    slots = max(2, (2 * look_dev + n_devices - 1) // n_devices)
-    owners = jnp.sum(jnp.where(lookup_table == table_ids[None, :], place[None, :], 0), axis=1)
-    hits = (owners[:, None] == jnp.arange(n_devices, dtype=jnp.int32)[None, :]).astype(jnp.int32)
-    earlier = jnp.cumsum(hits, axis=0) - hits
-    position = jnp.sum(earlier * hits, axis=1)
-    target = owners * slots + position
-    spread_unit = jnp.repeat(unit, LOOK_IMG, axis=0)
-    send_vec = jnp.zeros((n_devices * slots, proj_width), jnp.float32).at[target].set(spread_unit)
-    send_rows = jnp.full((n_devices * slots,), -1, jnp.int32).at[target].set(lookup_row)
-    got_vec, got_rows = (
-        core_and_chips(
-            send_vec.reshape(n_devices, slots, proj_width),
-            (("grp", "fsdp_0", "fsdp_1"), "fsdp_2"),
-            (1, 0),
-            0,
-            0,
-        ),
-        core_and_chips(
-            send_rows.reshape(n_devices, slots),
-            (("grp", "fsdp_0", "fsdp_1"), "fsdp_2"),
-            (1, 0),
-            0,
-            0,
-        ),
-    )
-    flat_rows = got_rows.reshape(-1)
-    valid = flat_rows >= 0
-    safe_rows = jnp.where(valid, flat_rows, 0)
-    diff = jnp.where(valid[:, None], local_table[safe_rows] - got_vec.reshape(-1, proj_width), 0.0)
-    grad_rows = jnp.zeros(local_table.shape, jnp.float32).at[safe_rows].add(diff)
-    returned = lax.all_to_all(
-        -diff.reshape(n_devices, slots, proj_width),
-        GRP_FSDP,
-        split_axis=0,
-        concat_axis=0,
-        tiled=True,
-    )
-    per_lookup = returned.reshape(-1, proj_width)[target]
-    grad_unit = jnp.sum(per_lookup.reshape(images, LOOK_IMG, proj_width), axis=1)
+    del scale, unit
+    everyone = lax.all_gather(pooled, GRP_FSDP, axis=0, tiled=True)
+    content_all = jnp.dot(everyone, w_proj, preferred_element_type=jnp.float32)
+    scale_all = lax.rsqrt(jnp.mean(content_all * content_all, axis=-1, keepdims=True) + epsilon)
+    unit_all = content_all * scale_all
+    grad_unit = LOOK_IMG * unit_all - row_sums
+    inner = jnp.mean(grad_unit * unit_all, axis=-1, keepdims=True)
+    grad_all = scale_all * (grad_unit - unit_all * inner)
+    content_grad = lax.dynamic_slice_in_dim(grad_all, images * me, images, axis=0)
+    share = width // n_devices
+    columns = lax.dynamic_slice_in_dim(everyone, share * me, share, axis=1).astype(jnp.float32)
+    proj_grad = jnp.dot(columns.T, grad_all, precision=lax.Precision.HIGHEST, preferred_element_type=jnp.float32)
+    named = jnp.sum(counts, axis=1, keepdims=True)
+    unit_sums = jnp.dot(counts, unit_all, precision=lax.Precision.HIGHEST, preferred_element_type=jnp.float32)
+    grad_rows = named * local_table - unit_sums
     accum_new = accum[0] + grad_rows * grad_rows
     table_new = local_table - learn_rate * grad_rows / jnp.sqrt(accum_new)
-    inner = jnp.mean(grad_unit * unit, axis=-1, keepdims=True)
-    content_grad = scale * (grad_unit - unit * inner)
-    share = width // n_devices
-    every_grad = lax.all_gather(content_grad, GRP_FSDP, axis=0, tiled=True)
-    my_columns = lax.all_to_all(
-        pooled.reshape(images, n_devices, share), GRP_FSDP, split_axis=1, concat_axis=0, tiled=True
-    )
-    column_block = my_columns.reshape(-1, share).astype(jnp.float32)
-    proj_grad = jnp.dot(
-        column_block.T,
-        every_grad,
-        precision=lax.Precision.HIGHEST,
-        preferred_element_type=jnp.float32,
-    )
     return (table_new[None], accum_new[None], content_grad, proj_grad)
 
 

time: 302 us -> 270 us (0.89)
  starting transfers between devices: 33.3 us -> 0.12 us
  waiting for transfers between devices: 56.4 us -> 26.8 us
  blocking collectives: 45.8 us -> 71 us
  matrix products: 64.1 us -> 76.3 us
  other arithmetic: 38.7 us -> 29.7 us
    all_gather x1 -> x2, blocking collectives: 37 us -> 71 us  [the longest x1 36.3 us: on_device(): everyone = lax.all_gather(pooled, GRP_FSDP, axis=0, tiled=True)]
    all_to_all x4 -> x0, starting transfers between devices: 33.3 us -> none  [the longest x2 19.8 us: turned_blocks(): lax.all_to_all(tiles, axes[k], split_axis=k, concat_axis=k, tiled=True)]
    all_gather x1, waiting for transfers between devices: 47.2 us -> 26.1 us  [sent_together(): out = lax.all_gather(both, axis, axis=dim, tiled=True)]
    dot_general x2 -> x4, matrix products: 1.12 us -> 13.1 us  [the longest x1 6.65 us: on_device(): lax.dot_general(counts, local_table, (((0,), (0,)), ((), ())), precision=...]
    unnamed x22 -> x20, local copies, waits for them, and re-layouts: 13 us -> 24.1 us
    all_to_all x2 -> x0, blocking collectives: 8.78 us -> none  [turned_blocks(): lax.all_to_all(tiles, axes[k], split_axis=k, concat_axis=k, tiled=True)]
    all_to_all x4 -> x0, waiting for transfers between devices: 8.47 us -> none  [the longest x2 6.97 us: turned_blocks(): lax.all_to_all(tiles, axes[k], split_axis=k, concat_axis=k, tiled=True)]
    broadcast_in_dim x1 -> x0, other arithmetic: 4.71 us -> none  [on_device(): return (table_new[None], accum_new[None], content_grad, proj_grad)]
  transfers between devices with their start and end apart: 6 -> 3, of which waited for: 4 -> 1; matrix products, arithmetic and copies ran while one was open for 43% -> 53% of each run, Pallas kernels for 0% -> 0%
where the time goes in v1:
time: 270 us; the launch traced here: 268 us
  matrix products  76.3 us (28%)
  blocking collectives  71 us (26%)
  local copies, waits for them, and re-layouts  48.5 us (18%)
  other arithmetic  29.7 us (11%)
  waiting for transfers between devices  26.8 us (10%)
  between operations  16 us (6%)
    all_gather x1, blocking collectives, on_device(): everyone = lax.all_gather(pooled, GRP_FSDP, axis=0, tiled=True)  36.3 us
    all_gather x1, blocking collectives, named_counts(): every = lax.all_gather(named[None, :], GRP_FSDP, axis=0, tiled=True)  34.7 us
    all_gather x1, waiting for transfers between devices, sent_together(): out = lax.all_gather(both, axis, axis=dim, tiled=True)  26.1 us
    dot_general x1, matrix products, on_device(): upward = jnp.dot(normed_two, full_up, preferred_element_type=jnp.float32)  26 us
    unnamed x20, local copies, waits for them, and re-layouts  24.1 us
    sub x1, other arithmetic, attend(): probs = jax.nn.softmax(scores, axis=-1).astype(jnp.bfloat16)  17.4 us
    dot_general x1, matrix products, attend(): jnp.einsum('bqhd,bkhd->bhqk', parts[:, :, 0], parts[:, :, 1], preferred_e...  9.96 us
    reshape x1, local copies, waits for them, and re-layouts, attend(): parts = qkv.reshape(images, seq, 3, HEADS, head_dim)  8.74 us
  transfers between devices with their start and end apart: 3, of which 1 were waited for; matrix products, arithmetic and copies ran while one was open for 53% of the time, Pallas kernels for 0%

profile of v1, /device:TPU:1, one launch (start us, length us, event | category | flops | bytes accessed | tf_op | source)
XLA Modules:
  0.0 268.4 jit_solution(11668020506386644739)
XLA Ops:
  8.0 0.0 copy-start
  8.0 0.0 copy-start.1
  8.0 0.0 all-gather.6.cloned.1.call-start
  8.1 2.0 pad_maximum_fusion
  10.0 0.0 all-gather.6.cloned.1.call-update
  10.1 0.0 all-gather.8.cloned.1.call-start
  10.1 0.7 all-gather.8.cloned.1.call-update
  10.8 0.0 all-reduce.2.cloned.1.call-start
  10.9 0.8 select_reduce_fusion
  11.7 0.7 fusion.83
  12.4 34.7 %all-gather.1 = s32[128,1,128]{2,1,0:T(1,128)S(1)} all-gather(s32[1,1,128]{2,1,0:T(1,128)S(1)} %fusion.83), channel_id=2, replica_groups=mesh['grp'=4,'fsdp_0'=4,'fsdp_1'=4,'fsdp_2'=2] {'grp','fsdp_0','fsdp_1',..., dimensions={0}, use_global_device_ids=true | all-gather | bytes 66048 | tf_op jit(solution)/shard_map/all_gather | solution.py:75
  47.1 0.1 fusion.76
  47.3 0.1 broadcast_in_dim.34
  47.3 0.1 eq.44
  47.5 0.1 broadcast_in_dim.33
  47.6 0.1 eq.41
  47.8 6.6 %fusion.36 = f32[256,256]{1,0:T(8,128)} fusion(f32[1,2048,256]{2,1,0:T(8,128)} %param.23, s32[256]{0:T(256)S(1)} %eq.44, s32[256]{0:T(256)S(1)} %eq.41, s32[256]{0:T(256)S(1)} %and_select_fusion.3, s32[2048]{0:T(1024)S(1)} %iota_multiply_fusion), kind=kOutput, calls=%fused_computation.51 | convolution fusion | flops 1613758464 | bytes 2370560 | tf_op jit(solution)/shard_map/dot_general | solution.py:113
  54.4 0.0 all-reduce.2.cloned.1.call-update
  54.4 0.0 copy-done.1
  54.4 1.7 copy.49
  56.1 0.9 convert_reduce_fusion.1
  57.0 0.0 copy-start.5
  57.0 1.5 multiply_reduce_fusion.2
  58.6 0.1 copy.65
  58.7 1.1 fusion.39
  59.8 2.0 reshape.114
  61.8 0.0 copy-start.2
  61.9 0.1 copy.66
  61.9 0.1 rsqrt.37
  62.0 0.1 div.60
  62.1 26.1 %all-gather.6.cloned.1.call-done = bf16[1024,8192]{1,0:T(8,128)(2,1)} async-done(((bf16[32,8192]{1,0:T(8,128)(2,1)}), bf16[1024,8192]{1,0:T(8,128)(2,1)}) %all-gather.6.cloned.1.call-update) | async-done | bytes 16777232 | tf_op jit(solution)/shard_map/all_gather | solution.py:22
  88.2 0.0 copy-done.5
  88.2 8.0 %fusion.20 = bf16[514,3072]{1,0:T(8,128)(2,1)} fusion(bf16[1024,8192]{1,0:T(8,128)(2,1)} %all-gather.6.cloned.1.call-done, f32[514,1024]{1,0:T(8,128)S(1)} %reshape.114, f32[1024]{0:T(1024)S(1)} %copy-done.5, f32[514]{0:T(1024)S(1)} %rsqrt.37, f32[514]{0:T(1024)S(1)} %div.60), kind=kOutput, calls=%fused_computation.30 | convolution fusion | flops 3237492736 | bytes 11563024 | tf_op jit(solution)/shard_map/dot_general | solution.py:121
  96.2 0.0 copy-done.2
  96.2 8.7 %reshape.125 = bf16[2,257,3,16,64]{4,3,2,1,0:T(8,128)(2,1)} reshape(bf16[514,3072]{1,0:T(8,128)(2,1)} %fusion.20) | data formatting | bytes 6316032 | tf_op jit(solution)/shard_map/reshape | solution.py:61
  104.9 6.1 %fusion.116 = (bf16[2,257,1,16,64]{4,3,2,1,0:T(8,128)(2,1)S(1)}, bf16[2,257,1,16,64]{4,3,2,1,0:T(8,128)(2,1)}, bf16[2,257,1,16,64]{4,3,2,1,0:T(8,128)(2,1)}) fusion(bf16[2,257,3,16,64]{4,3,2,1,0:T(8,128)(2,1)} %reshape.125), kind=kLoop, calls=%fused_computation.150 | loop fusion | bytes 6316032 | tf_op jit(solution)/shard_map/slice | solution.py:66
  111.1 4.3 %copy.63 = bf16[2,257,1,16,64]{1,4,3,0,2:T(8,128)(2,1)} copy(bf16[2,257,1,16,64]{4,3,2,1,0:T(8,128)(2,1)} %get-tuple-element.8) | data formatting | bytes 2105344
  115.4 4.3 %copy.64 = bf16[2,257,1,16,64]{1,4,3,0,2:T(8,128)(2,1)} copy(bf16[2,257,1,16,64]{4,3,2,1,0:T(8,128)(2,1)} %get-tuple-element.9) | data formatting | bytes 2105344
  119.7 10.0 %fusion.45 = f32[2,16,257,257]{2,3,1,0:T(8,128)} fusion(bf16[2,257,1,16,64]{1,4,3,0,2:T(8,128)(2,1)} %copy.64, bf16[2,257,1,16,64]{1,4,3,0,2:T(8,128)(2,1)} %copy.63), kind=kOutput, calls=%fused_computation.59 | convolution fusion | flops 270536704 | bytes 10559616 | tf_op jit(solution)/shard_map/bqhd,bkhd->bhqk/dot_general | solution.py:62
  129.6 17.4 %fusion.117 = (f32[2,16,257]{2,1,0:T(8,128)S(1)}, f32[2,16,257,257]{2,3,1,0:T(8,128)}) fusion(f32[2,16,257,257]{2,3,1,0:T(8,128)} %fusion.45), kind=kOutput, calls=%fused_computation.151 | output fusion | flops 8454528 | bytes 16941440 | tf_op jit(solution)/shard_map/sub | solution.py:65
  147.0 15.1 %copy.62 = bf16[2,257,1,16,64]{1,4,3,0,2:T(8,128)(2,1)} copy(bf16[2,257,1,16,64]{4,3,2,1,0:T(8,128)(2,1)S(1)} %get-tuple-element.7) | data formatting | bytes 2105344
  162.1 6.8 %fusion.49 = bf16[2,257,16,64]{1,3,2,0:T(8,128)(2,1)S(1)} fusion(f32[2,16,257,257]{2,3,1,0:T(8,128)} %get-tuple-element.13, f32[2,16,257]{2,1,0:T(8,128)S(1)} %get-tuple-element.12, bf16[2,257,1,16,64]{1,4,3,0,2:T(8,128)(2,1)} %copy.62), kind=kOutput, calls=%fused_computation.63 | convolution fusion | flops 275290176 | bytes 10592512 | tf_op jit(solution)/shard_map/bhqk,bkhd->bqhd/dot_general | solution.py:66
  168.9 1.6 copy.58
  170.5 1.2 reshape.112
  171.7 0.0 copy-start.6
  171.7 3.7 %convert_reduce_fusion = (f32[514]{0:T(1024)S(1)}, bf16[514,1024]{1,0:T(8,128)(2,1)S(1)}) fusion(f32[514,1024]{1,0:T(8,128)} %copy-done.2, bf16[514,1024]{0,1:T(8,128)(2,1)S(1)} %reshape.112, bf16[1024,8192]{1,0:T(8,128)(2,1)} %all-gather.6.cloned.1.call-done), kind=kOutput, calls=%fused_computation.34 | convolution fusion | flops 1080040960 | bytes 6334472 | tf_op jit(solution)/shard_map/dot_general | solution.py:123
  175.4 0.4 fusion.31
  175.9 0.0 copy-done.6
  175.9 26.0 %fusion.44.clone.4 = bf16[514,4096]{1,0:T(8,128)(2,1)} fusion(bf16[1024,8192]{1,0:T(8,128)(2,1)} %all-gather.6.cloned.1.call-done, bf16[514,1024]{1,0:T(8,128)(2,1)S(1)} %get-tuple-element.15, f32[1024]{0:T(1024)S(1)} %copy-done.6, f32[514]{0:T(1024)S(1)} %add_rsqrt_fusion.2, f32[514]{0:T(1024)S(1)} %broadcast_multiply_fusion.2), kind=kOutput, calls=%fused_computation.8.clone.clone.clone.clone.clone.clone.1 | convolution fusion | flops 4451223552 | bytes 13660176 | tf_op jit(solution)/shard_map/dot_general | solution.py:126
  201.9 8.7 %fusion.118 = (f32[514]{0:T(1024)S(1)}, f32[514,1024]{1,0:T(8,128)S(1)}) fusion(bf16[4096,1024]{1,0:T(8,128)(2,1)} %all-gather.8.cloned.1.call-done, bf16[514,1024]{1,0:T(8,128)(2,1)S(1)} %get-tuple-element.15, bf16[514,4096]{1,0:T(8,128)(2,1)} %fusion.44.clone.4), kind=kOutput, calls=%fused_computation.152 | convolution fusion | flops 4313323008 | bytes 15759368 | tf_op jit(solution)/shard_map/dot_general | solution.py:128
  210.7 0.4 multiply_reduce_fusion.1
  211.0 1.7 multiply_multiply_fusion.5
  212.7 1.8 reshape.113
  214.5 0.1 reduce_sum.127
  214.7 36.3 %all-gather.2 = bf16[128,2,1024]{2,1,0:T(2,128)(2,1)S(1)} all-gather(bf16[1,2,1024]{2,1,0:T(2,128)(2,1)S(1)} %fusion.81), channel_id=1, replica_groups=mesh['grp'=4,'fsdp_0'=4,'fsdp_1'=4,'fsdp_2'=2] {'grp','fsdp_0','fsdp_1',..., dimensions={0}, use_global_device_ids=true | all-gather | bytes 528384 | tf_op jit(solution)/shard_map/all_gather | solution.py:136
  251.0 0.2 reshape.121
  251.2 0.0 copy-start.3
  251.2 0.4 multiply_reduce_fusion.4
  251.6 0.0 all-reduce.2.cloned.1.call-done
  251.7 1.3 multiply_reduce_fusion.3
  253.0 1.1 subtract_multiply_fusion
  254.1 0.9 fusion.79
  255.0 0.6 constant_dynamic-slice_fusion
  255.6 5.2 %fusion.73 = (f32[1,2048,256]{2,1,0:T(8,128)}, f32[1,2048,256]{2,1,0:T(8,128)}) fusion(f32[1,2048,256]{2,1,0:T(8,128)S(1)} %copy-done.3, f32[1,2048,256]{2,1,0:T(8,128)} %param.23, f32[256,256]{1,0:T(8,128)S(1)} %get-tuple-element.19, f32[256]{0:T(256)S(1)} %add_rsqrt_fusion.3, s32[256]{0:T(256)S(1)} %eq.44, s32[256]{0:T(256)S(1)} %eq.41, ...), kind=kOutput, calls=%fused_computation.79 | convolution fusion | flops 1617494016 | bytes 8671232 | tf_op jit(solution)/shard_map/dot_general | solution.py:148
  (18 shorter events, 0.1 us)
Async XLA Ops:
  8.0 243.2 %copy-start = (bf16[1024,256]{1,0:T(8,128)(2,1)S(1)}, bf16[1024,256]{1,0:T(8,128)(2,1)}, u32[]{:S(2)}) copy-start(bf16[1024,256]{1,0:T(8,128)(2,1)} %param.22) | copy-start | bytes 1572868
  8.0 46.4 %copy-start.1 = (bf16[2,257,1024]{2,0,1:T(2,128)(2,1)S(1)}, bf16[2,257,1024]{2,0,1:T(2,128)(2,1)}, u32[]{:S(2)}) copy-start(bf16[2,257,1024]{2,0,1:T(2,128)(2,1)} %param.14) | copy-start | bytes 3158020
  8.0 80.1 %all-gather.6.cloned.1.call-start = ((), (), s32[]{:S(2)}) async-start(), calls=%async_computation | async-start | bytes 17301504 | tf_op jit(solution)/shard_map/all_gather | solution.py:22
  10.1 191.9 %all-gather.8.cloned.1.call-start = ((), (), s32[]{:S(2)}) async-start(), calls=%async_computation.1 | async-start | bytes 8650752 | tf_op jit(solution)/shard_map/all_gather | solution.py:118
  10.8 240.8 %all-reduce.2.cloned.1.call-start = ((), (), s32[]{:S(2)}) async-start(), calls=%async_computation.2 | async-start | bytes 524288 | tf_op jit(solution)/shard_map/psum | solution.py:112
  57.0 31.1 %copy-start.5 = (f32[1024]{0:T(1024)S(1)}, f32[1024]{0:T(1024)}, u32[]{:S(2)}) copy-start(f32[1024]{0:T(1024)} %param.15) | copy-start | bytes 12292
  61.8 34.4 %copy-start.2 = (f32[514,1024]{1,0:T(8,128)}, f32[514,1024]{1,0:T(8,128)S(1)}, u32[]{:S(2)}) copy-start(f32[514,1024]{1,0:T(8,128)S(1)} %reshape.114) | copy-start | bytes 6316036
  171.7 4.2 %copy-start.6 = (f32[1024]{0:T(1024)S(1)}, f32[1024]{0:T(1024)}, u32[]{:S(2)}) copy-start(f32[1024]{0:T(1024)} %param.18) | copy-start | bytes 12292
  201.9 9.1 %copy-start.4 = (f32[1024]{0:T(1024)S(1)}, f32[1024]{0:T(1024)}, u32[]{:S(2)}) copy-start(f32[1024]{0:T(1024)} %param.21) | copy-start | bytes 12292
  251.2 4.4 %copy-start.3 = (f32[1,2048,256]{2,1,0:T(8,128)S(1)}, f32[1,2048,256]{2,1,0:T(8,128)}, u32[]{:S(2)}) copy-start(f32[1,2048,256]{2,1,0:T(8,128)} %param.24) | copy-start | bytes 6291460
Sparse Core Ops, SparseCore 0:
  11.7 76.4 all-gather.5
  90.4 52.2 all-gather.7
Sparse Core Ops, SparseCore 1:
  54.5 161.8 all-reduce.1

commit v2 on v1

v2 whole, which is shorter than its diff:
```python
import functools

import jax
import jax.numpy as jnp
from jax import lax
from jax.experimental import pallas as pl
from jax.experimental.pallas import tpu as pltpu
from jax.sharding import Mesh
from jax.sharding import PartitionSpec as P

HEADS = 16
LOOK_IMG = 64
FSDP = ("fsdp_0", "fsdp_1", "fsdp_2")
GRP_FSDP = ("grp", "fsdp_0", "fsdp_1", "fsdp_2")
MESH = pl.DeviceIdType.MESH
PAD = 272
BLK = 32

epsilon = 1e-06
learn_rate = 0.5


def here():
    return tuple(lax.axis_index(a) for a in GRP_FSDP)


def moved(pos, axis, step):
    out = list(pos)
    out[axis] = lax.rem(pos[axis] + step, 2 if axis == 3 else 4)
    return tuple(out)


def wait_bytes(ref, sem):
    pltpu.make_async_copy(ref, ref, sem).wait()


class Weights:
    def __init__(self, own, full, sems, pos):
        self.own, self.full, self.sems = own, full, sems
        y, x, z, c = pos
        self.rows = own.shape[0]
        self.partner = (y, x, z, 1 - c)
        d = 1 - c
        self.i, self.j, self.c = x * d + z * c, z * d + x * c, c
        self.s1, self.s2 = 8 - 6 * c, 2 + 6 * c
        self.first = {k: (y, lax.rem(x + k * d, 4), lax.rem(z + k * c, 4), c) for k in (1, 3)}
        self.second = {k: (y, lax.rem(x + k * c, 4), lax.rem(z + k * d, 4), c) for k in (1, 3)}

    def part(self, di, dj, lo=0, size=None):
        size = self.rows if size is None else size
        block = lax.rem(self.i + di, 4) * self.s1 + lax.rem(self.j + dj, 4) * self.s2 + self.c
        return self.full.at[pl.ds(pl.multiple_of(block * self.rows + lo, 16), size)]

    def send(self, ref, sem, device, src=None):
        pltpu.make_async_remote_copy(
            src_ref=ref if src is None else src,
            dst_ref=ref,
            send_sem=self.sems.at[0],
            recv_sem=self.sems.at[sem],
            device_id=device,
            device_id_type=MESH,
        ).start()

    def got(self, ref, sem):
        wait_bytes(ref, self.sems.at[sem])

    def to_partner(self, ref, src=None):
        self.send(ref, 1, self.partner, src)

    def step0(self):
        mine = self.part(0, 0)
        pltpu.make_async_copy(self.own, mine, self.sems.at[2]).start()
        self.send(mine, 3, self.first[1], self.own)
        self.send(mine, 4, self.first[3], self.own)
        self.send(mine, 7, self.second[1], self.own)
        self.send(mine, 11, self.second[3], self.own)
        self.to_partner(mine, self.own)

    def spread(self, di, k):
        block = self.part(di, 0)
        self.send(block, 7 + k, self.second[1])
        self.send(block, 11 + k, self.second[3])
        self.to_partner(block)

    def step1(self):
        half = self.rows // 2
        self.got(self.part(3, 0), 3)
        self.send(self.part(3, 0, 0, half), 5, self.first[1])
        self.got(self.part(1, 0), 4)
        self.send(self.part(1, 0, half, half), 6, self.first[3])
        self.spread(3, 1)
        self.spread(1, 2)

    def step2(self):
        half = self.rows // 2
        self.got(self.part(2, 0, 0, half), 5)
        self.got(self.part(2, 0, half, half), 6)
        self.spread(2, 3)

    def pass_on(self, k, di):
        before, after = self.part(di, 3), self.part(di, 1)
        self.got(before, 7 + k)
        if k in (0, 2):
            self.send(before, 15 + k // 2, self.second[1])
        self.to_partner(before)
        self.got(after, 11 + k)
        if k in (1, 3):
            self.send(after, 17 + k // 2, self.second[3])
        self.to_partner(after)

    def step3(self):
        self.pass_on(0, 0)
        self.pass_on(1, 3)

    def step4(self):
        self.pass_on(2, 1)
        self.pass_on(3, 2)

    def step5(self):
        for sem, di in ((15, 0), (16, 1), (17, 3), (18, 2)):
            block = self.part(di, 2)
            self.got(block, sem)
            self.to_partner(block)

    def step6(self):
        self.got(self.full.at[pl.ds(0, 16 * self.rows)], 1)
        self.got(self.part(0, 0), 2)

    def finish(self):
        self.got(self.full.at[pl.ds(0, 31 * self.rows)], 0)

    def step(self, n):
        getattr(self, "step%d" % n)()


WEIGHT_SEMS = 19


class Spread:
    def __init__(self, buf, rows, sems, pos):
        self.buf, self.rows, self.sems, self.pos = buf, rows, sems, pos
        y, x, z, c = pos
        self.starts = (((c * 4 + z) * 4 + x) * 4 + y, ((c * 4 + z) * 4 + x) * 4, (c * 4 + z) * 16, c * 64)
        self.copies = {}

    def send(self, stage):
        axis, many = ((0, 1), (1, 4), (2, 16), (3, 64))[stage]
        part = self.buf.at[pl.ds(pl.multiple_of(self.starts[stage] * self.rows, 8), many * self.rows)]
        for k in (1,) if axis == 3 else (1, 2, 3):
            at = stage * 3 + k - 1
            copy = pltpu.make_async_remote_copy(
                src_ref=part,
                dst_ref=part,
                send_sem=self.sems.at[at],
                recv_sem=self.sems.at[10 + at],
                device_id=moved(self.pos, axis, k),
                device_id_type=MESH,
            )
            copy.start()
            self.copies.setdefault(stage, []).append(copy)

    def wait(self, stage):
        for copy in self.copies[stage]:
            copy.wait()


SPREAD_SEMS = 20


def exchange(pos, axis, sems, at, source, slots):
    copies = []
    for k in (1,) if axis == 3 else (1, 2, 3):
        copies.append(
            pltpu.make_async_remote_copy(
                src_ref=source(k),
                dst_ref=slots(k),
                send_sem=sems.at[at + k - 1],
                recv_sem=sems.at[at + 2 + k],
                device_id=moved(pos, axis, k),
                device_id_type=MESH,
            )
        )
    for copy in copies:
        copy.start()
    return copies


class RowSums:
    def __init__(self, part, total, from_core, from_axis, sems, pos):
        self.part, self.total, self.from_core, self.from_axis = part, total, from_core, from_axis
        self.sems, self.pos, self.copies = sems, pos, None
        y, x, z, c = pos
        self.half = pl.multiple_of(c * 64, 16)
        self.mine = pl.multiple_of(c * 64 + z * 16, 16)

    def send(self, stage):
        y, x, z, c = self.pos
        part, total = self.part, self.total
        if stage == 0:
            other = pl.ds(pl.multiple_of((1 - c) * 64, 16), 64)
            self.copies = exchange(self.pos, 3, self.sems, 0, lambda k: part.at[other], lambda k: self.from_core)
        if stage == 1:
            at = lambda k: part.at[pl.ds(pl.multiple_of(c * 64 + lax.rem(z + k, 4) * 16, 16), 16)]
            self.copies = exchange(self.pos, 2, self.sems, 6, at, lambda k: self.from_axis.at[0, k - 1])
        if stage in (2, 3):
            at = lambda k: part.at[pl.ds(self.mine, 16)] if stage == 2 else self.from_axis.at[3, 0]
            self.copies = exchange(
                self.pos, 3 - stage, self.sems, 6 * stage, at, lambda k: self.from_axis.at[stage - 1, k - 1]
            )
        if stage == 4:
            rows = lambda k: total.at[pl.ds(self.mine, 16)]
            self.copies = exchange(self.pos, 2, self.sems, 24, rows, rows)
        if stage == 5:
            rows = lambda k: total.at[pl.ds(self.half, 64)]
            self.copies = exchange(self.pos, 3, self.sems, 30, rows, rows)

    def wait(self, stage):
        for copy in self.copies:
            copy.wait()
        slots = self.from_axis
        if stage == 0:
            self.part[pl.ds(self.half, 64)] += self.from_core[...]
        if stage in (1, 2, 3):
            mine = slots[3, 0] if stage == 3 else self.part[pl.ds(self.mine, 16)]
            out = mine + slots[stage - 1, 0] + slots[stage - 1, 1] + slots[stage - 1, 2]
            if stage == 1:
                self.part[pl.ds(self.mine, 16)] = out
            if stage == 2:
                slots[3, 0] = out
            if stage == 3:
                self.total[pl.ds(self.mine, 16)] = out


SUMS_SEMS = 36


def normalized(values):
    center = jnp.mean(values, axis=-1, keepdims=True)
    shifted = values - center
    spread = jnp.mean(shifted * shifted, axis=-1, keepdims=True)
    return shifted * lax.rsqrt(spread + epsilon)


def two_parts(values):
    high = values.astype(jnp.bfloat16)
    return high, (values - high.astype(jnp.float32)).astype(jnp.bfloat16)


def split_dot(left, right):
    high, low = two_parts(right)
    return jnp.dot(left, high, preferred_element_type=jnp.float32) + jnp.dot(
        left, low, preferred_element_type=jnp.float32
    )


def gelu(v):
    return 0.5 * v * (1.0 + lax.erf(v * 0.7071067811865476))


def named_by(codes, column, base, rows, odd):
    wanted = (base + lax.broadcasted_iota(jnp.int32, (1, rows), 1)) * 2 + odd
    first, second = codes[:, column : column + 1], codes[:, column + 1 : column + 2]
    return (first == wanted).astype(jnp.float32) + (second == wanted).astype(jnp.float32)


def encoder(
    hidden,
    gain1,
    gain2,
    gain3,
    named,
    own_qkv,
    own_out,
    own_up,
    own_down,
    table,
    pooled_out,
    sums_out,
    codes_out,
    full_qkv,
    full_out,
    full_up,
    full_down,
    hid,
    norm,
    qkv,
    mixed,
    resid,
    act,
    final,
    named_all,
    pooled_all,
    pooled_f32,
    rows_table,
    part,
    from_core,
    from_axis,
    weight_sems,
    named_sems,
    pooled_sems,
    sums_sems,
    local_sem,
):
    pos = here()
    y, x, z, c = pos
    images, seq, width = hidden.shape
    me = ((y * 4 + x) * 4 + z) * 2 + c
    place = ((c * 4 + z) * 4 + x) * 4 + y
    load_table = pltpu.make_async_copy(table, rows_table, local_sem)
    load_table.start()
    barrier = pltpu.get_barrier_semaphore()
    peers = [moved(pos, axis, k) for axis in (0, 1, 2) for k in (1, 2, 3)] + [moved(pos, 3, 1)]
    for peer in peers:
        pl.semaphore_signal(barrier, inc=1, device_id=peer, device_id_type=MESH)
    named_all[pl.ds(pl.multiple_of(place * 8, 8), 8)] = named[...]
    pl.semaphore_wait(barrier, len(peers))

    A, B, C, D = (
        Weights(own, full, weight_sems.at[n], pos)
        for n, (own, full) in enumerate(
            ((own_qkv, full_qkv), (own_out, full_out), (own_up, full_up), (own_down, full_down))
        )
    )
    ids = Spread(named_all, 8, named_sems, pos)
    pools = Spread(pooled_all, 16, pooled_sems, pos)
    sums = RowSums(part, sums_out, from_core, from_axis, sums_sems, pos)

    ids.send(0)
    A.step(0)

    def load_rows(b, at, size):
        values = hidden[b, pl.ds(at, size), :].astype(jnp.float32)
        dst = pl.ds(pl.multiple_of(b * PAD + at, 16), size)
        norm[dst] = (normalized(values) * gain1[...]).astype(jnp.bfloat16)
        hid[dst] = values.astype(jnp.bfloat16)

    for b in range(images):
        lax.fori_loop(0, seq // BLK, lambda t, _: load_rows(b, pl.multiple_of(t * BLK, BLK), BLK), None)
        last = hidden[b, seq - 1 : seq, :].astype(jnp.float32)
        keep = lax.broadcasted_iota(jnp.int32, (16, 1), 0) == 0
        rows = jnp.where(keep, jnp.broadcast_to(last, (16, width)), 0.0)
        dst = pl.ds(b * PAD + seq - 1, 16)
        norm[dst] = (normalized(rows) * gain1[...]).astype(jnp.bfloat16)
        hid[dst] = rows.astype(jnp.bfloat16)
        if b == 0:
            ids.wait(0)
            ids.send(1)
            A.step(1)

    ids.wait(1)
    ids.send(2)
    A.step(2)
    B.step(0)
    ids.wait(2)
    ids.send(3)
    A.step(3)
    B.step(1)
    ids.wait(3)

    code = named_all[pl.ds(0, 128, stride=8), :] - me * 4096
    mine = (code >= 0) & (code < 4096)
    first = jnp.max(jnp.where(mine, code, -1), axis=1, keepdims=True)
    second = jnp.min(jnp.where(mine, code, 4096), axis=1, keepdims=True)
    many = jnp.sum(mine.astype(jnp.float32), axis=1, keepdims=True)
    second = jnp.where(many > 1.5, second, -1)
    lane = lax.broadcasted_iota(jnp.int32, (128, 128), 1)
    codes_out[...] = jnp.where(lane == 0, first, jnp.where(lane == 1, second, -1))
    A.step(4)
    B.step(2)
    load_table.wait()
    part[...] = jnp.zeros_like(part)

    def row_sums(n, _):
        codes = codes_out[...]
        high, low = two_parts(rows_table[pl.ds(pl.multiple_of(n * 256, 256), 256)])
        for b in range(2):
            hits = named_by(codes, 0, n * 256, 256, b).astype(jnp.bfloat16)
            part[:, 256 * b : 256 * b + 256] += jnp.dot(hits, high, preferred_element_type=jnp.float32) + jnp.dot(
                hits, low, preferred_element_type=jnp.float32
            )

    lax.fori_loop(0, 8, row_sums, None)
    sums.send(0)
    C.step(0)
    A.step(5)
    A.step(6)

    def project(n, _):
        at = pl.ds(pl.multiple_of(n * 256, 256), 256)
        qkv[:, at] = jnp.dot(norm[...], full_qkv[:, at], preferred_element_type=jnp.float32).astype(jnp.bfloat16)

    lax.fori_loop(0, 4, project, None)
    B.step(3)
    C.step(1)
    sums.wait(0)
    sums.send(1)
    lax.fori_loop(4, 8, project, None)
    B.step(4)
    C.step(2)
    sums.wait(1)
    sums.send(2)
    lax.fori_loop(8, 12, project, None)
    B.step(5)
    sums.wait(2)
    sums.send(3)

    lower = lax.broadcasted_iota(jnp.int32, (1, 128), 1) < 64

    def attend(n, _):
        b, pair = n // 8, lax.rem(n, 8)
        top = pl.multiple_of(b * PAD, 16)
        at = [pl.ds(pl.multiple_of(pair * 128 + part_at, 128), 128) for part_at in (0, width, 2 * width)]
        query = qkv[pl.ds(top, PAD), at[0]]
        keys = qkv[pl.ds(top, 256), at[1]]
        values = qkv[pl.ds(top, 256), at[2]]
        last = pl.ds(pl.multiple_of(top + 256, 16), 16)
        last_key = qkv[last, at[1]].astype(jnp.float32)[0:1]
        last_value = qkv[last, at[2]].astype(jnp.float32)[0:1]
        with_last = query.astype(jnp.float32) * last_key
        outs = []
        for side in (lower, jnp.logical_not(lower)):
            chosen = jnp.where(side, query.astype(jnp.float32) * 0.125, 0.0).astype(jnp.bfloat16)
            scores = lax.dot_general(chosen, keys, (((1,), (1,)), ((), ())), preferred_element_type=jnp.float32)
            extra = jnp.sum(jnp.where(side, with_last, 0.0), axis=-1, keepdims=True) * 0.125
            top_score = jnp.maximum(jnp.max(scores, axis=-1, keepdims=True), extra)
            probs = jnp.exp(scores - top_score)
            extra = jnp.exp(extra - top_score)
            share = 1.0 / (jnp.sum(probs, axis=-1, keepdims=True) + extra)
            out = jnp.dot(probs.astype(jnp.bfloat16), values, preferred_element_type=jnp.float32)
            outs.append((out + extra * last_value) * share)
        mixed[pl.ds(top, PAD), at[0]] = jnp.where(lower, outs[0], outs[1]).astype(jnp.bfloat16)

    lax.fori_loop(0, 4, attend, None)
    C.step(3)
    B.step(6)
    sums.wait(3)
    sums.send(4)
    lax.fori_loop(4, 8, attend, None)
    C.step(4)
    D.step(0)
    sums.wait(4)
    sums.send(5)
    lax.fori_loop(8, 12, attend, None)
    C.step(5)
    D.step(1)
    sums.wait(5)
    lax.fori_loop(12, 16, attend, None)
    D.step(2)

    def out_project(n, _):
        at = pl.ds(pl.multiple_of(n * 256, 256), 256)
        add = jnp.dot(mixed[...], full_out[:, at], preferred_element_type=jnp.float32)
        resid[:, at] = (hid[:, at].astype(jnp.float32) + add).astype(jnp.bfloat16)

    lax.fori_loop(0, 4, out_project, None)

    def second_norm(n, _):
        at = pl.ds(pl.multiple_of(n * BLK, BLK), BLK)
        norm[at] = (normalized(resid[at].astype(jnp.float32)) * gain2[...]).astype(jnp.bfloat16)

    lax.fori_loop(0, 2 * PAD // BLK, second_norm, None)
    C.step(6)
    D.step(3)

    def up_project(n, _):
        at = pl.ds(pl.multiple_of(n * 256, 256), 256)
        act[:, at] = gelu(jnp.dot(norm[...], full_up[:, at], preferred_element_type=jnp.float32)).astype(jnp.bfloat16)

    lax.fori_loop(0, 5, up_project, None)
    D.step(4)
    lax.fori_loop(5, 10, up_project, None)
    D.step(5)
    lax.fori_loop(10, 16, up_project, None)
    D.step(6)

    def down_project(n, _):
        at = pl.ds(pl.multiple_of(n * 256, 256), 256)
        add = jnp.dot(act[...], full_down[:, at], preferred_element_type=jnp.float32)
        final[:, at] = resid[:, at].astype(jnp.float32) + add

    lax.fori_loop(0, 4, down_project, None)

    pieces = []
    for b in range(images):

        def pool(t, total):
            rows = normalized(final[pl.ds(pl.multiple_of(b * PAD + t * BLK, 16), BLK)])
            return total + jnp.sum(rows.reshape(BLK // 8, 8, width), axis=0)

        total = lax.fori_loop(0, seq // BLK, pool, jnp.zeros((8, width), jnp.float32))
        rows = normalized(final[pl.ds(b * PAD + seq - 1, 8)])
        keep = lax.broadcasted_iota(jnp.int32, (8, 1), 0) == 0
        total = jnp.sum(total + jnp.where(keep, rows, 0.0), axis=0, keepdims=True) * gain3[...] * (1.0 / seq)
        pieces.extend(total[:, 128 * n : 128 * n + 128] for n in range(width // 128))
    pooled_all[pl.ds(pl.multiple_of(place * 16, 16), 16)] = jnp.concatenate(pieces, axis=0).astype(jnp.bfloat16)
    for stage in range(4):
        pools.send(stage)
        pools.wait(stage)
    pooled_f32[...] = pooled_all[...].astype(jnp.float32)
    for b in range(2):
        for n in range(8):
            rows = pooled_f32[pl.ds(b * 8 + n, 128, stride=16), :]
            pooled_out[128 * b : 128 * b + 128, 128 * n : 128 * n + 128] = rows.astype(jnp.bfloat16)
    for weight in (A, B, C, D):
        weight.finish()


def encode(hidden, gain1, gain2, gain3, named, own, table):
    images, seq, width = hidden.shape
    rows = 2 * PAD
    sizes = [(w.shape[0] * 32, w.shape[1]) for w in own]
    bf16, f32 = jnp.bfloat16, jnp.float32
    vmem = pl.BlockSpec(memory_space=pltpu.VMEM)
    anywhere = pl.BlockSpec(memory_space=pl.ANY)
    return pl.pallas_call(
        encoder,
        out_shape=(
            jax.ShapeDtypeStruct((256, width), bf16),
            jax.ShapeDtypeStruct((128, 512), f32),
            jax.ShapeDtypeStruct((128, 128), jnp.int32),
        ),
        in_specs=[vmem] * 5 + [anywhere] * 5,
        out_specs=(vmem,) * 3,
        scratch_shapes=[pltpu.VMEM(s, bf16) for s in sizes]
        + [
            pltpu.VMEM((rows, width), bf16),
            pltpu.VMEM((rows, width), bf16),
            pltpu.VMEM((rows, 3 * width), bf16),
            pltpu.VMEM((rows, width), bf16),
            pltpu.VMEM((rows, width), bf16),
            pltpu.VMEM((rows, 4 * width), bf16),
            pltpu.VMEM((rows, width), f32),
            pltpu.VMEM((1024, 128), jnp.int32),
            pltpu.VMEM((2048, 128), bf16),
            pltpu.VMEM((2048, 128), f32),
            pltpu.VMEM(table.shape, f32),
            pltpu.VMEM((128, 512), f32),
            pltpu.VMEM((64, 512), f32),
            pltpu.VMEM((4, 3, 16, 512), f32),
            pltpu.SemaphoreType.DMA((4, WEIGHT_SEMS)),
            pltpu.SemaphoreType.DMA((SPREAD_SEMS,)),
            pltpu.SemaphoreType.DMA((SPREAD_SEMS,)),
            pltpu.SemaphoreType.DMA((SUMS_SEMS,)),
            pltpu.SemaphoreType.DMA,
        ],
        compiler_params=pltpu.CompilerParams(
            collective_id=0, has_side_effects=True, vmem_limit_bytes=58 * 1024 * 1024
        ),
        name="encoder",
    )(hidden, gain1, gain2, gain3, named, *own, table)


def align(pooled, w_proj, sums, codes, table, accum, table_new, accum_new, content_grad, proj_grad, unit, grads, columns):
    step = pl.program_id(0)

    @pl.when(step == 0)
    def _():
        y, x, z, c = here()
        me = ((y * 4 + x) * 4 + z) * 2 + c
        place = ((c * 4 + z) * 4 + x) * 4 + y
        content = jnp.dot(pooled[...], w_proj[...], preferred_element_type=jnp.float32)
        scale = lax.rsqrt(jnp.mean(content * content, axis=-1, keepdims=True) + epsilon)
        units = content * scale
        unit[...] = units
        both = jnp.concatenate([sums[:, 0:256], sums[:, 256:512]], axis=0)
        grad_unit = LOOK_IMG * units - both
        inner = jnp.mean(grad_unit * units, axis=-1, keepdims=True)
        grads[...] = scale * (grad_unit - units * inner)
        content_grad[0:1] = grads[pl.ds(place, 1)]
        content_grad[1:2] = grads[pl.ds(place + 128, 1)]
        lanes = pl.ds(pl.multiple_of(me // 16 * 128, 128), 128)
        high, low = two_parts(grads[...])
        turned = lambda right: lax.dot_general(
            pooled[:, lanes], right, (((0,), (0,)), ((), ())), preferred_element_type=jnp.float32
        )
        columns[...] = turned(high) + turned(low)
        proj_grad[...] = columns[pl.ds(pl.multiple_of(lax.rem(me, 16) * 8, 8), 8)]

    rows = table.shape[0]
    base = step * rows
    pairs = codes[...]
    hits = jnp.concatenate([named_by(pairs, 0, base, rows, b) for b in range(2)], axis=0)
    named = lax.dot_general(
        hits.astype(jnp.bfloat16),
        jnp.ones((256, 128), jnp.bfloat16),
        (((0,), (0,)), ((), ())),
        preferred_element_type=jnp.float32,
    )[:, 0:1]
    high, low = two_parts(unit[...])
    turned = lambda right: lax.dot_general(
        hits.astype(jnp.bfloat16), right, (((0,), (0,)), ((), ())), preferred_element_type=jnp.float32
    )
    grad_rows = named * table[...] - (turned(high) + turned(low))
    fresh = accum[...] + grad_rows * grad_rows
    accum_new[...] = fresh
    table_new[...] = table[...] - learn_rate * grad_rows / jnp.sqrt(fresh)


def finish(pooled, w_proj, sums, codes, table, accum):
    n, width = table.shape
    rows = 512
    whole = lambda a: pl.BlockSpec(a.shape, lambda i: (0, 0))
    tiles = pl.BlockSpec((rows, width), lambda i: (i, 0))
    f32 = jnp.float32
    return pl.pallas_call(
        align,
        grid=(n // rows,),
        out_shape=(
            jax.ShapeDtypeStruct(table.shape, f32),
            jax.ShapeDtypeStruct(table.shape, f32),
            jax.ShapeDtypeStruct((2, 256), f32),
            jax.ShapeDtypeStruct((8, 256), f32),
        ),
        in_specs=[whole(pooled), whole(w_proj), whole(sums), whole(codes), tiles, tiles],
        out_specs=(
            tiles,
            tiles,
            pl.BlockSpec((2, 256), lambda i: (0, 0)),
            pl.BlockSpec((8, 256), lambda i: (0, 0)),
        ),
        scratch_shapes=[pltpu.VMEM((256, 256), f32), pltpu.VMEM((256, 256), f32), pltpu.VMEM((128, 256), f32)],
        compiler_params=pltpu.CompilerParams(dimension_semantics=("arbitrary",)),
        name="align",
    )(pooled, w_proj, sums, codes, table, accum)


def on_device(
    hidden,
    ln1_gain,
    w_qkv,
    w_out,
    ln2_gain,
    w_up,
    w_down,
    post_gain,
    w_proj,
    table,
    accum,
    place,
    lookup_table,
    lookup_row,
):
    images = hidden.shape[0]
    rows_dev = table.shape[1]
    table_ids = jnp.arange(place.shape[0], dtype=jnp.int32)
    owners = jnp.sum(jnp.where(lookup_table == table_ids[None, :], place[None, :], 0), axis=1)
    image = jnp.arange(lookup_row.shape[0], dtype=jnp.int32) // LOOK_IMG
    named = (owners * rows_dev + lookup_row) * images + image
    named = jnp.broadcast_to(named[None, :], (8, named.shape[0]))
    pooled, sums, codes = encode(
        hidden,
        ln1_gain[None, :],
        ln2_gain[None, :],
        post_gain[None, :],
        named,
        (w_qkv, w_out, w_up, w_down),
        table[0],
    )
    table_new, accum_new, content_grad, proj_grad = finish(pooled, w_proj, sums, codes, table[0], accum[0])
    return (table_new[None], accum_new[None], content_grad, proj_grad)


def solution(mesh):
    torus = Mesh(
        mesh.devices.reshape(mesh.shape["grp"], 4, 4, 2), ("grp", "fsdp_0", "fsdp_1", "fsdp_2")
    )
    in_specs = (
        P(GRP_FSDP, None, None),
        P(),
        P(FSDP, None),
        P(FSDP, None),
        P(),
        P(FSDP, None),
        P(FSDP, None),
        P(),
        P(),
        P(GRP_FSDP, None, None),
        P(GRP_FSDP, None, None),
        P(),
        P(GRP_FSDP, None),
        P(GRP_FSDP),
    )
    out_specs = (
        P(GRP_FSDP, None, None),
        P(GRP_FSDP, None, None),
        P(GRP_FSDP, None),
        P(GRP_FSDP, None),
    )
    return jax.shard_map(
        on_device, mesh=torus, in_specs=in_specs, out_specs=out_specs, check_vma=False
    )
```

time: 270 us -> 131 us (0.49)
  Pallas kernels: 0 us -> 125 us
  matrix products: 76.3 us -> 0 us
  blocking collectives: 71 us -> 0 us
  local copies, waits for them, and re-layouts: 48.5 us -> 3.08 us
  other arithmetic: 29.7 us -> 1.51 us
  waiting for transfers between devices: 26.8 us -> 0 us
  between operations: 16 us -> 0.65 us
    pallas_call x0 -> x2, Pallas kernels: none -> 125 us  [the longest x1 118 us: encode(): pl.pallas_call(encoder, out_shape=(jax.ShapeDtypeStruct((256, width), bf1...]
    dot_general x10 -> x0, matrix products: 76.3 us -> none  [the longest x1 26 us: on_device(): upward = jnp.dot(normed_two, full_up, preferred_element_type=jnp.float32)]
    all_gather x2 -> x0, blocking collectives: 71 us -> none  [the longest x1 36.3 us: on_device(): everyone = lax.all_gather(pooled, GRP_FSDP, axis=0, tiled=True)]
    all_gather x2 -> x0, waiting for transfers between devices: 26.1 us -> none  [the longest x1 26.1 us: sent_together(): out = lax.all_gather(both, axis, axis=dim, tiled=True)]
    unnamed x20 -> x1, local copies, waits for them, and re-layouts: 24.1 us -> 2.48 us
    sub x2 -> x0, other arithmetic: 17.4 us -> none  [the longest x1 17.4 us: attend(): probs = jax.nn.softmax(scores, axis=-1).astype(jnp.bfloat16)]
    reshape x3 -> x0, local copies, waits for them, and re-layouts: 11.8 us -> none  [the longest x1 8.74 us: attend(): parts = qkv.reshape(images, seq, 3, HEADS, head_dim)]
    slice x1 -> x0, local copies, waits for them, and re-layouts: 6.11 us -> none  [attend(): parts[:, :, 2]]
  transfers between devices with their start and end apart: 3 -> 0, of which waited for: 1 -> 0; matrix products, arithmetic and copies ran while one was open for 53% -> 0% of each run, Pallas kernels for 0% -> 0%
where the time goes in v2:
time: 131 us; the launch traced here: 130 us
  Pallas kernels  125 us (95%)
  local copies, waits for them, and re-layouts  3.08 us (2%)
  other arithmetic  1.51 us (1%)
    pallas_call x1, Pallas kernels, encode(): pl.pallas_call(encoder, out_shape=(jax.ShapeDtypeStruct((256, width), bf1...  118 us
    pallas_call x1, Pallas kernels, finish(): pl.pallas_call(align, grid=(n // rows,), out_shape=(jax.ShapeDtypeStruct(...  7.05 us

profile of v2, /device:TPU:1, one launch (start us, length us, event | category | flops | bytes accessed | tf_op | source)
XLA Modules:
  0.0 130.4 jit_solution(4775419790709770987)
XLA Ops:
  0.6 0.8 select_reduce_fusion
  1.5 0.7 fusion
  2.1 0.6 broadcast_in_dim.40.named
  2.7 2.5 %copy.19.hidden = bf16[2,257,1024]{2,1,0:T(8,128)(2,1)} copy(bf16[2,257,1024]{2,0,1:T(2,128)(2,1)} %param.14) | data formatting | bytes 2105344 | tf_op args[0]
  5.2 118.2 %encoder.1 = (bf16[256,1024]{1,0:T(8,128)(2,1)}, f32[128,512]{1,0:T(8,128)}, s32[128,128]{1,0:T(8,128)}) custom-call(bf16[2,257,1024]{2,1,0:T(8,128)(2,1)} %copy.19.hidden, f32[1,1024]{1,0:T(1,128)} %bitcast.11, f32[1,1024]{1,0:T(1,128)} %bitcast.12, f32[1,1024]{1,0:T(1,128)} %bitcast.13, s32[8,128]{1,0:T(8,128)} %broadcast_in_dim.40.named, ...), custom_call_target="tpu_custom_call" | custom-call | tf_op jit(solution)/shard_map/encoder/pallas_call | solution.py:515
  123.4 7.0 %align.1 = (f32[2048,256]{1,0:T(8,128)}, f32[2048,256]{1,0:T(8,128)}, f32[2,256]{1,0:T(2,128)}, f32[8,256]{1,0:T(8,128)}) custom-call(bf16[256,1024]{1,0:T(8,128)(2,1)} %get-tuple-element.11.pooled, bf16[1024,256]{1,0:T(8,128)(2,1)} %w_proj.1, f32[128,512]{1,0:T(8,128)} %get-tuple-element.12.sums, s32[128,128]{1,0:T(8,128)} %get-tuple-element.13.codes, ...), custom_call_target="tpu_custom_call" | custom-call | tf_op jit(solution)/shard_map/align/pallas_call | solution.py:605

commit v3 on v2

--- a/solution.py
+++ b/solution.py
@@ -38,7 +38,7 @@
     def __init__(self, own, full, sems, pos):
         self.own, self.full, self.sems = own, full, sems
         y, x, z, c = pos
-        self.rows = own.shape[0]
+        self.rows = own[0].shape[0]
         self.partner = (y, x, z, 1 - c)
         d = 1 - c
         self.i, self.j, self.c = x * d + z * c, z * d + x * c, c
@@ -46,16 +46,27 @@
         self.first = {k: (y, lax.rem(x + k * d, 4), lax.rem(z + k * c, 4), c) for k in (1, 3)}
         self.second = {k: (y, lax.rem(x + k * c, 4), lax.rem(z + k * d, 4), c) for k in (1, 3)}
 
+    def span(self, start, size):
+        if len(self.full.shape) == 3:
+            return self.full.at[:, pl.ds(start, size)]
+        return self.full.at[pl.ds(start, size)]
+
     def part(self, di, dj, lo=0, size=None):
         size = self.rows if size is None else size
         block = lax.rem(self.i + di, 4) * self.s1 + lax.rem(self.j + dj, 4) * self.s2 + self.c
-        return self.full.at[pl.ds(pl.multiple_of(block * self.rows + lo, 16), size)]
-
-    def send(self, ref, sem, device, src=None):
+        return self.span(pl.multiple_of(block * self.rows + lo, 16), size)
+
+    def fetch(self):
+        mine = self.part(0, 0)
+        for n, own in enumerate(self.own):
+            to = mine.at[n] if len(self.own) > 1 else mine
+            pltpu.make_async_copy(own, to, self.sems.at[2]).start()
+
+    def send(self, ref, sem, device):
         pltpu.make_async_remote_copy(
-            src_ref=ref if src is None else src,
+            src_ref=ref,
             dst_ref=ref,
-            send_sem=self.sems.at[0],
+            send_sem=self.sems.at[19 if sem == 1 else 0],
             recv_sem=self.sems.at[sem],
             device_id=device,
             device_id_type=MESH,
@@ -64,17 +75,20 @@
     def got(self, ref, sem):
         wait_bytes(ref, self.sems.at[sem])
 
-    def to_partner(self, ref, src=None):
-        self.send(ref, 1, self.partner, src)
-
-    def step0(self):
+    def to_partner(self, ref):
+        self.send(ref, 1, self.partner)
+
+    def start(self):
         mine = self.part(0, 0)
-        pltpu.make_async_copy(self.own, mine, self.sems.at[2]).start()
-        self.send(mine, 3, self.first[1], self.own)
-        self.send(mine, 4, self.first[3], self.own)
-        self.send(mine, 7, self.second[1], self.own)
-        self.send(mine, 11, self.second[3], self.own)
-        self.to_partner(mine, self.own)
+        self.got(mine, 2)
+        self.send(mine, 3, self.first[1])
+        self.send(mine, 4, self.first[3])
+        self.to_partner(mine)
+
+    def send_own(self):
+        mine = self.part(0, 0)
+        self.send(mine, 7, self.second[1])
+        self.send(mine, 11, self.second[3])
 
     def spread(self, di, k):
         block = self.part(di, 0)
@@ -82,58 +96,130 @@
         self.send(block, 11 + k, self.second[3])
         self.to_partner(block)
 
-    def step1(self):
+    def from_before(self):
         half = self.rows // 2
         self.got(self.part(3, 0), 3)
         self.send(self.part(3, 0, 0, half), 5, self.first[1])
+        self.spread(3, 1)
+
+    def from_after(self):
+        half = self.rows // 2
         self.got(self.part(1, 0), 4)
         self.send(self.part(1, 0, half, half), 6, self.first[3])
-        self.spread(3, 1)
         self.spread(1, 2)
 
-    def step2(self):
+    def opposite(self):
         half = self.rows // 2
         self.got(self.part(2, 0, 0, half), 5)
         self.got(self.part(2, 0, half, half), 6)
         self.spread(2, 3)
 
-    def pass_on(self, k, di):
-        before, after = self.part(di, 3), self.part(di, 1)
-        self.got(before, 7 + k)
+    def column_before(self, k):
+        block = self.part(ORDER[k], 3)
+        self.got(block, 7 + k)
         if k in (0, 2):
-            self.send(before, 15 + k // 2, self.second[1])
-        self.to_partner(before)
-        self.got(after, 11 + k)
+            self.send(block, 15 + k // 2, self.second[1])
+        self.to_partner(block)
+
+    def column_after(self, k):
+        block = self.part(ORDER[k], 1)
+        self.got(block, 11 + k)
         if k in (1, 3):
-            self.send(after, 17 + k // 2, self.second[3])
-        self.to_partner(after)
-
-    def step3(self):
-        self.pass_on(0, 0)
-        self.pass_on(1, 3)
-
-    def step4(self):
-        self.pass_on(2, 1)
-        self.pass_on(3, 2)
-
-    def step5(self):
-        for sem, di in ((15, 0), (16, 1), (17, 3), (18, 2)):
-            block = self.part(di, 2)
-            self.got(block, sem)
-            self.to_partner(block)
-
-    def step6(self):
-        self.got(self.full.at[pl.ds(0, 16 * self.rows)], 1)
-        self.got(self.part(0, 0), 2)
+            self.send(block, 17 + k // 2, self.second[3])
+        self.to_partner(block)
+
+    def column_opposite(self, k):
+        block = self.part(ORDER[k], 2)
+        self.got(block, (15, 17, 16, 18)[k])
+        self.to_partner(block)
+
+    def complete(self):
+        self.got(self.span(0, 16 * self.rows), 1)
 
     def finish(self):
-        self.got(self.full.at[pl.ds(0, 31 * self.rows)], 0)
-
-    def step(self, n):
-        getattr(self, "step%d" % n)()
-
-
-WEIGHT_SEMS = 19
+        self.got(self.span(0, 16 * self.rows), 19)
+        self.got(self.span(0, 15 * self.rows), 0)
+
+    def step(self, *names):
+        named = {"start": self.start, "own": self.send_own, "f-": self.from_before, "f+": self.from_after}
+        named.update({"h": self.opposite, "end": self.complete})
+        grouped = {"b": self.column_before, "a": self.column_after, "o": self.column_opposite, "y": self.across_step}
+        for name in names:
+            if name in named:
+                named[name]()
+            else:
+                grouped[name[0]](name[1] if name[0] == "y" else int(name[1]))
+
+    def across_step(self, name):
+        raise NotImplementedError
+
+
+ORDER = (0, 3, 1, 2)
+WEIGHT_SEMS = 20
+
+
+class Quarters(Weights):
+    def __init__(self, own, full, sems, more, pos):
+        y, x, z, c = pos
+        rows = full.shape[3]
+        super().__init__((own.at[pl.ds(pl.multiple_of(y * rows, 16), rows)],), full, sems, pos)
+        self.y, self.more = y, more
+        self.t1, self.t2 = 4 - 3 * c, 1 + 3 * c
+        self.up, self.down = moved(pos, 0, 1), moved(pos, 0, 3)
+
+    def part(self, di, dj, lo=0, size=None):
+        size = self.rows if size is None else size
+        block = lax.rem(self.i + di, 4) * self.t1 + lax.rem(self.j + dj, 4) * self.t2
+        return self.full.at[block, self.c, self.y, pl.ds(lo, size)]
+
+    def quarter(self, dy):
+        return self.full.at[:, self.c, lax.rem(self.y + dy, 4)]
+
+    def half(self, dy, lo):
+        return self.full.at[pl.ds(lo, 8), self.c, lax.rem(self.y + dy, 4)]
+
+    def across(self, ref, sem, device):
+        pltpu.make_async_remote_copy(
+            src_ref=ref,
+            dst_ref=ref,
+            send_sem=self.more.at[sem],
+            recv_sem=self.more.at[7 + sem],
+            device_id=device,
+            device_id_type=MESH,
+        ).start()
+
+    def across_step(self, name):
+        if name == "0":
+            self.across(self.quarter(0), 0, self.up)
+            self.across(self.quarter(0), 1, self.down)
+        if name == "-":
+            wait_bytes(self.quarter(3), self.more.at[7])
+            self.across(self.half(3, 0), 2, self.up)
+            self.across(self.quarter(3), 4, self.partner)
+        if name == "+":
+            wait_bytes(self.quarter(1), self.more.at[8])
+            self.across(self.half(1, 8), 3, self.down)
+            self.across(self.quarter(1), 5, self.partner)
+        if name == "2":
+            wait_bytes(self.half(2, 0), self.more.at[9])
+            wait_bytes(self.half(2, 8), self.more.at[10])
+            self.across(self.quarter(2), 6, self.partner)
+
+    def complete(self):
+        self.got(self.full.at[:, 0, 0], 1)
+        for sem in (4, 5, 6):
+            wait_bytes(self.quarter(0), self.more.at[7 + sem])
+
+    def finish(self):
+        self.got(self.full.at[:, 0, 0], 19)
+        self.got(self.full.at[pl.ds(0, 15), 0, 0], 0)
+        for sem in (0, 1, 4, 5, 6):
+            wait_bytes(self.quarter(0), self.more.at[sem])
+        for sem in (2, 3):
+            wait_bytes(self.half(0, 0), self.more.at[sem])
+
+
+QUARTER_SEMS = 14
 
 
 class Spread:
@@ -268,7 +354,9 @@
     gain1,
     gain2,
     gain3,
-    named,
+    tables,
+    table_rows,
+    places,
     own_qkv,
     own_out,
     own_up,
@@ -277,9 +365,11 @@
     pooled_out,
     sums_out,
     codes_out,
-    full_qkv,
+    full_qkv1,
+    full_qkv2,
     full_out,
-    full_up,
+    full_up1,
+    full_up2,
     full_down,
     hid,
     norm,
@@ -296,6 +386,7 @@
     from_core,
     from_axis,
     weight_sems,
+    quarter_sems,
     named_sems,
     pooled_sems,
     sums_sems,
@@ -303,111 +394,97 @@
 ):
     pos = here()
     y, x, z, c = pos
-    images, seq, width = hidden.shape
+    seq, images, width = hidden.shape
     me = ((y * 4 + x) * 4 + z) * 2 + c
-    place = ((c * 4 + z) * 4 + x) * 4 + y
+    me_place = ((c * 4 + z) * 4 + x) * 4 + y
+    third = lambda half: [own_qkv.at[:, pl.ds(n * width + half * (width // 2), width // 2)] for n in range(3)]
+    A1, A2, B, C1, C2 = (
+        Weights(own, full, weight_sems.at[n], pos)
+        for n, (own, full) in enumerate(
+            (
+                (third(0), full_qkv1),
+                (third(1), full_qkv2),
+                ([own_out], full_out),
+                ([own_up.at[:, pl.ds(0, 2 * width)]], full_up1),
+                ([own_up.at[:, pl.ds(2 * width, 2 * width)]], full_up2),
+            )
+        )
+    )
+    D = Quarters(own_down, full_down, weight_sems.at[5], quarter_sems, pos)
+    for weight in (D, A1, A2, B, C1, C2):
+        weight.fetch()
     load_table = pltpu.make_async_copy(table, rows_table, local_sem)
     load_table.start()
     barrier = pltpu.get_barrier_semaphore()
     peers = [moved(pos, axis, k) for axis in (0, 1, 2) for k in (1, 2, 3)] + [moved(pos, 3, 1)]
     for peer in peers:
         pl.semaphore_signal(barrier, inc=1, device_id=peer, device_id_type=MESH)
-    named_all[pl.ds(pl.multiple_of(place * 8, 8), 8)] = named[...]
+    down_rows = lax.broadcasted_iota(jnp.int32, (128, 128), 0)
+    along = lax.broadcasted_iota(jnp.int32, (128, 128), 1)
+    turned_place = jnp.sum(jnp.where(down_rows == along, places[...], 0).astype(jnp.float32), axis=1, keepdims=True)
+    owners = jnp.sum(jnp.where(down_rows == tables[...], turned_place, 0.0), axis=0, keepdims=True)
+    image = along[0:1] // LOOK_IMG
+    named = (owners.astype(jnp.int32) * 2048 + table_rows[...]) * 2 + image
+    named_all[pl.ds(pl.multiple_of(me_place * 8, 8), 8)] = jnp.broadcast_to(named, (8, 128))
     pl.semaphore_wait(barrier, len(peers))
 
-    A, B, C, D = (
-        Weights(own, full, weight_sems.at[n], pos)
-        for n, (own, full) in enumerate(
-            ((own_qkv, full_qkv), (own_out, full_out), (own_up, full_up), (own_down, full_down))
-        )
-    )
     ids = Spread(named_all, 8, named_sems, pos)
     pools = Spread(pooled_all, 16, pooled_sems, pos)
     sums = RowSums(part, sums_out, from_core, from_axis, sums_sems, pos)
 
-    ids.send(0)
-    A.step(0)
-
     def load_rows(b, at, size):
-        values = hidden[b, pl.ds(at, size), :].astype(jnp.float32)
+        values = hidden[pl.ds(at, size), b, :].astype(jnp.float32)
         dst = pl.ds(pl.multiple_of(b * PAD + at, 16), size)
         norm[dst] = (normalized(values) * gain1[...]).astype(jnp.bfloat16)
         hid[dst] = values.astype(jnp.bfloat16)
 
-    for b in range(images):
-        lax.fori_loop(0, seq // BLK, lambda t, _: load_rows(b, pl.multiple_of(t * BLK, BLK), BLK), None)
-        last = hidden[b, seq - 1 : seq, :].astype(jnp.float32)
+    def load(b, start, end):
+        lax.fori_loop(start, end, lambda t, _: load_rows(b, pl.multiple_of(t * BLK, BLK), BLK), None)
+        if end < seq // BLK:
+            return
+        last = hidden[seq - 1 : seq, b, :].astype(jnp.float32)
         keep = lax.broadcasted_iota(jnp.int32, (16, 1), 0) == 0
         rows = jnp.where(keep, jnp.broadcast_to(last, (16, width)), 0.0)
         dst = pl.ds(b * PAD + seq - 1, 16)
         norm[dst] = (normalized(rows) * gain1[...]).astype(jnp.bfloat16)
         hid[dst] = rows.astype(jnp.bfloat16)
-        if b == 0:
-            ids.wait(0)
-            ids.send(1)
-            A.step(1)
-
-    ids.wait(1)
-    ids.send(2)
-    A.step(2)
-    B.step(0)
-    ids.wait(2)
-    ids.send(3)
-    A.step(3)
-    B.step(1)
-    ids.wait(3)
-
-    code = named_all[pl.ds(0, 128, stride=8), :] - me * 4096
-    mine = (code >= 0) & (code < 4096)
-    first = jnp.max(jnp.where(mine, code, -1), axis=1, keepdims=True)
-    second = jnp.min(jnp.where(mine, code, 4096), axis=1, keepdims=True)
-    many = jnp.sum(mine.astype(jnp.float32), axis=1, keepdims=True)
-    second = jnp.where(many > 1.5, second, -1)
-    lane = lax.broadcasted_iota(jnp.int32, (128, 128), 1)
-    codes_out[...] = jnp.where(lane == 0, first, jnp.where(lane == 1, second, -1))
-    A.step(4)
-    B.step(2)
-    load_table.wait()
-    part[...] = jnp.zeros_like(part)
-
-    def row_sums(n, _):
-        codes = codes_out[...]
-        high, low = two_parts(rows_table[pl.ds(pl.multiple_of(n * 256, 256), 256)])
-        for b in range(2):
-            hits = named_by(codes, 0, n * 256, 256, b).astype(jnp.bfloat16)
-            part[:, 256 * b : 256 * b + 256] += jnp.dot(hits, high, preferred_element_type=jnp.float32) + jnp.dot(
-                hits, low, preferred_element_type=jnp.float32
-            )
-
-    lax.fori_loop(0, 8, row_sums, None)
-    sums.send(0)
-    C.step(0)
-    A.step(5)
-    A.step(6)
-
-    def project(n, _):
-        at = pl.ds(pl.multiple_of(n * 256, 256), 256)
-        qkv[:, at] = jnp.dot(norm[...], full_qkv[:, at], preferred_element_type=jnp.float32).astype(jnp.bfloat16)
-
-    lax.fori_loop(0, 4, project, None)
-    B.step(3)
-    C.step(1)
-    sums.wait(0)
-    sums.send(1)
-    lax.fori_loop(4, 8, project, None)
-    B.step(4)
-    C.step(2)
-    sums.wait(1)
-    sums.send(2)
-    lax.fori_loop(8, 12, project, None)
-    B.step(5)
-    sums.wait(2)
-    sums.send(3)
+
+    def name_rows():
+        code = named_all[pl.ds(0, 128, stride=8), :] - me * 4096
+        mine = (code >= 0) & (code < 4096)
+        first = jnp.max(jnp.where(mine, code, -1), axis=1, keepdims=True)
+        second = jnp.min(jnp.where(mine, code, 4096), axis=1, keepdims=True)
+        many = jnp.sum(mine.astype(jnp.float32), axis=1, keepdims=True)
+        second = jnp.where(many > 1.5, second, -1)
+        lane = lax.broadcasted_iota(jnp.int32, (128, 128), 1)
+        codes = jnp.where(lane == 0, first, jnp.where(lane == 1, second, -1))
+        in_rows = [
+            jnp.sum(jnp.where(down_rows == along, v, 0).astype(jnp.float32), axis=0, keepdims=True) for v in (first, second)
+        ]
+        codes_out[...] = jnp.concatenate(in_rows + [jnp.zeros((6, 128), jnp.float32)], axis=0).astype(jnp.int32)
+        load_table.wait()
+        part[...] = jnp.zeros_like(part)
+
+        def row_sums(n, _):
+            high, low = two_parts(rows_table[pl.ds(pl.multiple_of(n * 256, 256), 256)])
+            for b in range(2):
+                hits = named_by(codes, 0, n * 256, 256, b).astype(jnp.bfloat16)
+                part[:, 256 * b : 256 * b + 256] += jnp.dot(hits, high, preferred_element_type=jnp.float32) + jnp.dot(
+                    hits, low, preferred_element_type=jnp.float32
+                )
+
+        lax.fori_loop(0, 8, row_sums, None)
+
+    def project(half, n, _):
+        third, tile = n // 2, lax.rem(n, 2) * 256
+        weight = (full_qkv1, full_qkv2)[half][third, :, pl.ds(pl.multiple_of(tile, 256), 256)]
+        at = pl.ds(pl.multiple_of(third * width + half * (width // 2) + tile, 256), 256)
+        qkv[:, at] = jnp.dot(norm[...], weight, preferred_element_type=jnp.float32).astype(jnp.bfloat16)
 
     lower = lax.broadcasted_iota(jnp.int32, (1, 128), 1) < 64
 
-    def attend(n, _):
-        b, pair = n // 8, lax.rem(n, 8)
+    def attend(half, n, _):
+        b, pair = n // 4, half * 4 + lax.rem(n, 4)
         top = pl.multiple_of(b * PAD, 16)
         at = [pl.ds(pl.multiple_of(pair * 128 + part_at, 128), 128) for part_at in (0, width, 2 * width)]
         query = qkv[pl.ds(top, PAD), at[0]]
@@ -430,55 +507,145 @@
             outs.append((out + extra * last_value) * share)
         mixed[pl.ds(top, PAD), at[0]] = jnp.where(lower, outs[0], outs[1]).astype(jnp.bfloat16)
 
-    lax.fori_loop(0, 4, attend, None)
-    C.step(3)
-    B.step(6)
-    sums.wait(3)
-    sums.send(4)
-    lax.fori_loop(4, 8, attend, None)
-    C.step(4)
-    D.step(0)
-    sums.wait(4)
-    sums.send(5)
-    lax.fori_loop(8, 12, attend, None)
-    C.step(5)
-    D.step(1)
-    sums.wait(5)
-    lax.fori_loop(12, 16, attend, None)
-    D.step(2)
-
     def out_project(n, _):
         at = pl.ds(pl.multiple_of(n * 256, 256), 256)
         add = jnp.dot(mixed[...], full_out[:, at], preferred_element_type=jnp.float32)
         resid[:, at] = (hid[:, at].astype(jnp.float32) + add).astype(jnp.bfloat16)
 
-    lax.fori_loop(0, 4, out_project, None)
-
     def second_norm(n, _):
         at = pl.ds(pl.multiple_of(n * BLK, BLK), BLK)
         norm[at] = (normalized(resid[at].astype(jnp.float32)) * gain2[...]).astype(jnp.bfloat16)
 
-    lax.fori_loop(0, 2 * PAD // BLK, second_norm, None)
-    C.step(6)
-    D.step(3)
-
-    def up_project(n, _):
+    def up_project(piece, n, _):
+        here_at = pl.ds(pl.multiple_of(n * 256, 256), 256)
+        at = pl.ds(pl.multiple_of(piece * 2 * width + n * 256, 256), 256)
+        up = jnp.dot(norm[...], (full_up1, full_up2)[piece][:, here_at], preferred_element_type=jnp.float32)
+        act[:, at] = gelu(up).astype(jnp.bfloat16)
+
+    def down_project(piece, n, _):
         at = pl.ds(pl.multiple_of(n * 256, 256), 256)
-        act[:, at] = gelu(jnp.dot(norm[...], full_up[:, at], preferred_element_type=jnp.float32)).astype(jnp.bfloat16)
-
-    lax.fori_loop(0, 5, up_project, None)
-    D.step(4)
-    lax.fori_loop(5, 10, up_project, None)
-    D.step(5)
-    lax.fori_loop(10, 16, up_project, None)
-    D.step(6)
-
-    def down_project(n, _):
-        at = pl.ds(pl.multiple_of(n * 256, 256), 256)
-        add = jnp.dot(act[...], full_down[:, at], preferred_element_type=jnp.float32)
-        final[:, at] = resid[:, at].astype(jnp.float32) + add
-
-    lax.fori_loop(0, 4, down_project, None)
+        weight = full_down[pl.ds(piece * 8, 8), :, :, :, at].reshape(2 * width, 256)
+        before = resid[:, at].astype(jnp.float32) if piece == 0 else final[:, at]
+        left = act[:, pl.ds(piece * 2 * width, 2 * width)]
+        final[:, at] = before + jnp.dot(left, weight, preferred_element_type=jnp.float32)
+
+    run = lambda body, start, end: lax.fori_loop(start, end, body, None)
+
+    D.step("start")
+    A1.step("start")
+    D.step("own")
+    A1.step("own")
+    ids.send(0)
+    load(0, 0, 8)
+    D.step("f-", "f+")
+    load(1, 0, 4)
+    D.step("b0", "a0")
+    load(1, 4, 8)
+    A1.step("f-")
+    D.step("h")
+    A1.step("f+")
+    D.step("b1", "a1")
+    A1.step("b0", "a0")
+    D.step("b2", "a2", "o0")
+    ids.wait(0)
+    ids.send(1)
+    A1.step("h", "b1", "a1")
+    D.step("b3", "a3")
+    A1.step("b2", "a2")
+    D.step("o1")
+    A1.step("o0")
+    D.step("o2")
+    A1.step("a3")
+    A2.step("start", "own")
+    A1.step("b3", "o1")
+    D.step("o3", "y0")
+    A1.step("o2", "o3")
+    A2.step("f-", "f+", "b0")
+    ids.wait(1)
+    A2.step("a0")
+    ids.send(2)
+    A1.step("end")
+    run(functools.partial(project, 0), 0, 4)
+    A2.step("h", "b1", "a1")
+    run(functools.partial(project, 0), 4, 6)
+    A2.step("b2", "a2")
+    run(functools.partial(attend, 0), 0, 2)
+    A2.step("o0")
+    B.step("start")
+    C1.step("start")
+    A2.step("b3", "a3")
+    B.step("own")
+    C1.step("own")
+    A2.step("o1")
+    run(functools.partial(attend, 0), 2, 4)
+    A2.step("o2")
+    run(functools.partial(attend, 0), 4, 6)
+    B.step("f-", "f+", "b0")
+    ids.wait(2)
+    A2.step("o3")
+    ids.send(3)
+    run(functools.partial(attend, 0), 6, 8)
+    B.step("a0")
+    C1.step("f-", "f+")
+    B.step("h")
+    C1.step("b0")
+    B.step("b1")
+    A2.step("end")
+    run(functools.partial(project, 1), 0, 2)
+    B.step("a1", "b2")
+    C1.step("a0")
+    run(functools.partial(project, 1), 2, 4)
+    C2.step("start")
+    B.step("a2", "o0")
+    C1.step("h")
+    C2.step("own")
+    C1.step("b1")
+    ids.wait(3)
+    name_rows()
+    B.step("b3")
+    C1.step("a1", "b2", "a2")
+    sums.send(0)
+    run(functools.partial(project, 1), 4, 6)
+    D.step("y-", "y+")
+    B.step("a3", "o1")
+    C1.step("o0")
+    C2.step("f-")
+    B.step("o2")
+    C2.step("f+")
+    C1.step("a3")
+    sums.wait(0)
+    sums.send(1)
+    run(functools.partial(attend, 1), 0, 2)
+    C1.step("b3")
+    C2.step("a0")
+    run(functools.partial(attend, 1), 2, 4)
+    C2.step("h")
+    C1.step("o1")
+    C2.step("b0")
+    run(functools.partial(attend, 1), 4, 6)
+    B.step("o3")
+    C1.step("o2")
+    run(functools.partial(attend, 1), 6, 8)
+    C2.step("b1", "a1")
+    B.step("end")
+    run(out_project, 0, 4)
+    C1.step("o3")
+    C2.step("b2", "a2", "b3")
+    sums.wait(1)
+    run(second_norm, 0, 2 * PAD // BLK)
+    C2.step("a3", "o0", "o1")
+    C1.step("end")
+    run(functools.partial(up_project, 0), 0, 2)
+    D.step("y2")
+    C2.step("o2")
+    run(functools.partial(up_project, 0), 2, 6)
+    C2.step("o3")
+    run(functools.partial(up_project, 0), 6, 8)
+    D.step("end")
+    run(functools.partial(down_project, 0), 0, 4)
+    C2.step("end")
+    run(functools.partial(up_project, 1), 0, 8)
+    run(functools.partial(down_project, 1), 0, 4)
 
     pieces = []
     for b in range(images):
@@ -492,23 +659,26 @@
         keep = lax.broadcasted_iota(jnp.int32, (8, 1), 0) == 0
         total = jnp.sum(total + jnp.where(keep, rows, 0.0), axis=0, keepdims=True) * gain3[...] * (1.0 / seq)
         pieces.extend(total[:, 128 * n : 128 * n + 128] for n in range(width // 128))
-    pooled_all[pl.ds(pl.multiple_of(place * 16, 16), 16)] = jnp.concatenate(pieces, axis=0).astype(jnp.bfloat16)
+    pooled_all[pl.ds(pl.multiple_of(me_place * 16, 16), 16)] = jnp.concatenate(pieces, axis=0).astype(jnp.bfloat16)
     for stage in range(4):
         pools.send(stage)
+        sums.send(stage + 2)
+        sums.wait(stage + 2)
         pools.wait(stage)
     pooled_f32[...] = pooled_all[...].astype(jnp.float32)
     for b in range(2):
         for n in range(8):
             rows = pooled_f32[pl.ds(b * 8 + n, 128, stride=16), :]
             pooled_out[128 * b : 128 * b + 128, 128 * n : 128 * n + 128] = rows.astype(jnp.bfloat16)
-    for weight in (A, B, C, D):
+    for weight in (A1, A2, B, C1, C2, D):
         weight.finish()
 
 
-def encode(hidden, gain1, gain2, gain3, named, own, table):
-    images, seq, width = hidden.shape
+def encode(hidden, gains, lookups, own, table):
+    width = hidden.shape[2]
     rows = 2 * PAD
-    sizes = [(w.shape[0] * 32, w.shape[1]) for w in own]
+    sizes = [(3, width, width // 2)] * 2 + [(width, width)] + [(width, 2 * width)] * 2
+    sizes.append((16, 2, 4, own[3].shape[0] // 4, width))
     bf16, f32 = jnp.bfloat16, jnp.float32
     vmem = pl.BlockSpec(memory_space=pltpu.VMEM)
     anywhere = pl.BlockSpec(memory_space=pl.ANY)
@@ -517,9 +687,9 @@
         out_shape=(
             jax.ShapeDtypeStruct((256, width), bf16),
             jax.ShapeDtypeStruct((128, 512), f32),
-            jax.ShapeDtypeStruct((128, 128), jnp.int32),
+            jax.ShapeDtypeStruct((8, 128), jnp.int32),
         ),
-        in_specs=[vmem] * 5 + [anywhere] * 5,
+        in_specs=[vmem] * 7 + [anywhere] * 5,
         out_specs=(vmem,) * 3,
         scratch_shapes=[pltpu.VMEM(s, bf16) for s in sizes]
         + [
@@ -537,7 +707,8 @@
             pltpu.VMEM((128, 512), f32),
             pltpu.VMEM((64, 512), f32),
             pltpu.VMEM((4, 3, 16, 512), f32),
-            pltpu.SemaphoreType.DMA((4, WEIGHT_SEMS)),
+            pltpu.SemaphoreType.DMA((6, WEIGHT_SEMS)),
+            pltpu.SemaphoreType.DMA((QUARTER_SEMS,)),
             pltpu.SemaphoreType.DMA((SPREAD_SEMS,)),
             pltpu.SemaphoreType.DMA((SPREAD_SEMS,)),
             pltpu.SemaphoreType.DMA((SUMS_SEMS,)),
@@ -547,7 +718,7 @@
             collective_id=0, has_side_effects=True, vmem_limit_bytes=58 * 1024 * 1024
         ),
         name="encoder",
-    )(hidden, gain1, gain2, gain3, named, *own, table)
+    )(hidden, *gains, *lookups, *own, table)
 
 
 def align(pooled, w_proj, sums, codes, table, accum, table_new, accum_new, content_grad, proj_grad, unit, grads, columns):
@@ -578,19 +749,13 @@
 
     rows = table.shape[0]
     base = step * rows
-    pairs = codes[...]
-    hits = jnp.concatenate([named_by(pairs, 0, base, rows, b) for b in range(2)], axis=0)
-    named = lax.dot_general(
-        hits.astype(jnp.bfloat16),
-        jnp.ones((256, 128), jnp.bfloat16),
-        (((0,), (0,)), ((), ())),
-        preferred_element_type=jnp.float32,
-    )[:, 0:1]
-    high, low = two_parts(unit[...])
-    turned = lambda right: lax.dot_general(
-        hits.astype(jnp.bfloat16), right, (((0,), (0,)), ((), ())), preferred_element_type=jnp.float32
-    )
-    grad_rows = named * table[...] - (turned(high) + turned(low))
+    wanted = (base + lax.broadcasted_iota(jnp.int32, (rows, 1), 0)) * 2
+    hits = [
+        (codes[0:1] == wanted + b).astype(jnp.float32) + (codes[1:2] == wanted + b).astype(jnp.float32) for b in range(2)
+    ]
+    hits = jnp.concatenate(hits, axis=1).astype(jnp.bfloat16)
+    named = jnp.dot(hits, jnp.ones((256, 128), jnp.bfloat16), preferred_element_type=jnp.float32)[:, 0:1]
+    grad_rows = named * table[...] - split_dot(hits, unit[...])
     fresh = accum[...] + grad_rows * grad_rows
     accum_new[...] = fresh
     table_new[...] = table[...] - learn_rate * grad_rows / jnp.sqrt(fresh)
@@ -640,19 +805,10 @@
     lookup_table,
     lookup_row,
 ):
-    images = hidden.shape[0]
-    rows_dev = table.shape[1]
-    table_ids = jnp.arange(place.shape[0], dtype=jnp.int32)
-    owners = jnp.sum(jnp.where(lookup_table == table_ids[None, :], place[None, :], 0), axis=1)
-    image = jnp.arange(lookup_row.shape[0], dtype=jnp.int32) // LOOK_IMG
-    named = (owners * rows_dev + lookup_row) * images + image
-    named = jnp.broadcast_to(named[None, :], (8, named.shape[0]))
     pooled, sums, codes = encode(
-        hidden,
-        ln1_gain[None, :],
-        ln2_gain[None, :],
-        post_gain[None, :],
-        named,
+        jnp.swapaxes(hidden, 0, 1),
+        (ln1_gain[None, :], ln2_gain[None, :], post_gain[None, :]),
+        (lookup_table.reshape(1, -1), lookup_row[None, :], place[None, :]),
         (w_qkv, w_out, w_up, w_down),
         table[0],
     )

time: 131 us -> 115 us (0.88)
  Pallas kernels: 125 us -> 114 us
  local copies, waits for them, and re-layouts: 3.08 us -> 0 us
  other arithmetic: 1.51 us -> 0 us
    pallas_call x1, Pallas kernels: 118 us -> 107 us  [encode(): pl.pallas_call(encoder, out_shape=(jax.ShapeDtypeStruct((256, width), bf1...]
    unnamed x1 -> x0, local copies, waits for them, and re-layouts: 2.48 us -> none
where the time goes in v3:
time: 115 us; the launch traced here: 114 us
  Pallas kernels  114 us (99%)
    pallas_call x1, Pallas kernels, encode(): pl.pallas_call(encoder, out_shape=(jax.ShapeDtypeStruct((256, width), bf1...  107 us
    pallas_call x1, Pallas kernels, finish(): pl.pallas_call(align, grid=(n // rows,), out_shape=(jax.ShapeDtypeStruct(...  6.83 us

profile of v3, /device:TPU:1, one launch (start us, length us, event | category | flops | bytes accessed | tf_op | source)
XLA Modules:
  0.0 114.3 jit_solution(417452407280852889)
XLA Ops:
  0.6 106.9 %encoder.1 = (bf16[256,1024]{1,0:T(8,128)(2,1)}, f32[128,512]{1,0:T(8,128)}, s32[8,128]{1,0:T(8,128)}) custom-call(bf16[257,2,1024]{2,1,0:T(2,128)(2,1)} %bitcast.14, f32[1,1024]{1,0:T(1,128)} %bitcast.15, f32[1,1024]{1,0:T(1,128)} %bitcast.16, f32[1,1024]{1,0:T(1,128)} %bitcast.17, s32[1,128]{1,0:T(1,128)} %bitcast.18, s32[1,128]{1,0:T(1,128)} %bitcast.19, ...), custom_call_target="tpu_custom_call" | custom-call | tf_op jit(solution)/shard_map/encoder/pallas_call | solution.py:685
  107.5 6.8 %align.1 = (f32[2048,256]{1,0:T(8,128)}, f32[2048,256]{1,0:T(8,128)}, f32[2,256]{1,0:T(2,128)}, f32[8,256]{1,0:T(8,128)}) custom-call(bf16[256,1024]{1,0:T(8,128)(2,1)} %get-tuple-element.11.pooled, bf16[1024,256]{1,0:T(8,128)(2,1)} %w_proj.1, f32[128,512]{1,0:T(8,128)} %get-tuple-element.12.sums, s32[8,128]{1,0:T(8,128)} %get-tuple-element.13.codes, ...), custom_call_target="tpu_custom_call" | custom-call | tf_op jit(solution)/shard_map/align/pallas_call | solution.py:770

commit v4 on v3

--- a/solution.py
+++ b/solution.py
@@ -332,13 +332,6 @@
     return high, (values - high.astype(jnp.float32)).astype(jnp.bfloat16)
 
 
-def split_dot(left, right):
-    high, low = two_parts(right)
-    return jnp.dot(left, high, preferred_element_type=jnp.float32) + jnp.dot(
-        left, low, preferred_element_type=jnp.float32
-    )
-
-
 def gelu(v):
     return 0.5 * v * (1.0 + lax.erf(v * 0.7071067811865476))
 
@@ -350,21 +343,29 @@
 
 
 def encoder(
-    hidden,
     gain1,
     gain2,
     gain3,
     tables,
     table_rows,
     places,
+    hidden_in,
+    proj_in,
     own_qkv,
     own_out,
     own_up,
     own_down,
     table,
-    pooled_out,
-    sums_out,
+    unit_high,
+    unit_low,
     codes_out,
+    content_grad,
+    proj_grad,
+    hidden,
+    proj,
+    total_sums,
+    grads,
+    columns,
     full_qkv1,
     full_qkv2,
     full_out,
@@ -390,7 +391,7 @@
     named_sems,
     pooled_sems,
     sums_sems,
-    local_sem,
+    local_sems,
 ):
     pos = here()
     y, x, z, c = pos
@@ -413,8 +414,12 @@
     D = Quarters(own_down, full_down, weight_sems.at[5], quarter_sems, pos)
     for weight in (D, A1, A2, B, C1, C2):
         weight.fetch()
-    load_table = pltpu.make_async_copy(table, rows_table, local_sem)
+    load_hidden = pltpu.make_async_copy(hidden_in, hidden, local_sems.at[0])
+    load_hidden.start()
+    load_table = pltpu.make_async_copy(table, rows_table, local_sems.at[1])
     load_table.start()
+    load_proj = pltpu.make_async_copy(proj_in, proj, local_sems.at[2])
+    load_proj.start()
     barrier = pltpu.get_barrier_semaphore()
     peers = [moved(pos, axis, k) for axis in (0, 1, 2) for k in (1, 2, 3)] + [moved(pos, 3, 1)]
     for peer in peers:
@@ -430,7 +435,7 @@
 
     ids = Spread(named_all, 8, named_sems, pos)
     pools = Spread(pooled_all, 16, pooled_sems, pos)
-    sums = RowSums(part, sums_out, from_core, from_axis, sums_sems, pos)
+    sums = RowSums(part, total_sums, from_core, from_axis, sums_sems, pos)
 
     def load_rows(b, at, size):
         values = hidden[pl.ds(at, size), b, :].astype(jnp.float32)
@@ -536,6 +541,7 @@
     D.step("own")
     A1.step("own")
     ids.send(0)
+    load_hidden.wait()
     load(0, 0, 8)
     D.step("f-", "f+")
     load(1, 0, 4)
@@ -554,98 +560,105 @@
     A1.step("b2", "a2")
     D.step("o1")
     A1.step("o0")
+    A2.step("start")
     D.step("o2")
     A1.step("a3")
-    A2.step("start", "own")
-    A1.step("b3", "o1")
+    B.step("start")
+    A2.step("own")
+    A1.step("b3")
+    B.step("own")
+    A1.step("o1")
     D.step("o3", "y0")
-    A1.step("o2", "o3")
-    A2.step("f-", "f+", "b0")
+    A1.step("o2")
+    A2.step("f-", "f+")
+    A1.step("o3")
+    B.step("f-")
+    A2.step("b0")
     ids.wait(1)
+    B.step("f+", "b0")
+    ids.send(2)
     A2.step("a0")
-    ids.send(2)
     A1.step("end")
-    run(functools.partial(project, 0), 0, 4)
-    A2.step("h", "b1", "a1")
+    run(functools.partial(project, 0), 0, 2)
+    A2.step("h", "b1")
+    B.step("a0")
+    run(functools.partial(project, 0), 2, 4)
+    A2.step("a1", "b2")
+    B.step("h", "b1")
     run(functools.partial(project, 0), 4, 6)
-    A2.step("b2", "a2")
+    A2.step("a2", "o0")
+    B.step("a1", "b2", "a2")
     run(functools.partial(attend, 0), 0, 2)
-    A2.step("o0")
-    B.step("start")
     C1.step("start")
-    A2.step("b3", "a3")
-    B.step("own")
+    A2.step("a3", "b3")
+    B.step("o0")
+    C2.step("start")
+    A2.step("o1")
     C1.step("own")
-    A2.step("o1")
+    C2.step("own")
+    A2.step("o2")
+    B.step("a3")
     run(functools.partial(attend, 0), 2, 4)
-    A2.step("o2")
+    B.step("b3", "o1")
+    ids.wait(2)
+    ids.send(3)
     run(functools.partial(attend, 0), 4, 6)
-    B.step("f-", "f+", "b0")
-    ids.wait(2)
     A2.step("o3")
-    ids.send(3)
+    B.step("o2")
     run(functools.partial(attend, 0), 6, 8)
-    B.step("a0")
-    C1.step("f-", "f+")
-    B.step("h")
-    C1.step("b0")
-    B.step("b1")
+    C1.step("f-", "f+", "b0")
     A2.step("end")
     run(functools.partial(project, 1), 0, 2)
-    B.step("a1", "b2")
     C1.step("a0")
-    run(functools.partial(project, 1), 2, 4)
-    C2.step("start")
-    B.step("a2", "o0")
-    C1.step("h")
-    C2.step("own")
-    C1.step("b1")
+    C2.step("f-", "f+")
     ids.wait(3)
     name_rows()
-    B.step("b3")
-    C1.step("a1", "b2", "a2")
+    B.step("o3")
+    C1.step("h", "b1")
+    C2.step("h", "b0", "a0")
     sums.send(0)
-    run(functools.partial(project, 1), 4, 6)
+    C1.step("a1")
+    run(functools.partial(project, 1), 2, 4)
+    C1.step("b2", "a2")
     D.step("y-", "y+")
-    B.step("a3", "o1")
     C1.step("o0")
-    C2.step("f-")
-    B.step("o2")
-    C2.step("f+")
-    C1.step("a3")
     sums.wait(0)
     sums.send(1)
+    run(functools.partial(project, 1), 4, 6)
+    C2.step("b1", "a1")
     run(functools.partial(attend, 1), 0, 2)
-    C1.step("b3")
-    C2.step("a0")
+    C2.step("b2", "a2")
     run(functools.partial(attend, 1), 2, 4)
-    C2.step("h")
+    C1.step("b3", "a3")
+    run(functools.partial(attend, 1), 4, 6)
+    C2.step("b3", "a3")
+    run(functools.partial(attend, 1), 6, 8)
     C1.step("o1")
-    C2.step("b0")
-    run(functools.partial(attend, 1), 4, 6)
-    B.step("o3")
-    C1.step("o2")
-    run(functools.partial(attend, 1), 6, 8)
-    C2.step("b1", "a1")
+    C2.step("o0")
     B.step("end")
     run(out_project, 0, 4)
-    C1.step("o3")
-    C2.step("b2", "a2", "b3")
+    C1.step("o2", "o3")
+    C2.step("o1", "o2")
+    run(second_norm, 0, 2 * PAD // BLK)
+    C2.step("o3")
+    C1.step("end")
     sums.wait(1)
-    run(second_norm, 0, 2 * PAD // BLK)
-    C2.step("a3", "o0", "o1")
-    C1.step("end")
+    sums.send(2)
     run(functools.partial(up_project, 0), 0, 2)
     D.step("y2")
-    C2.step("o2")
-    run(functools.partial(up_project, 0), 2, 6)
-    C2.step("o3")
-    run(functools.partial(up_project, 0), 6, 8)
+    run(functools.partial(up_project, 0), 2, 8)
     D.step("end")
+    sums.wait(2)
+    sums.send(3)
     run(functools.partial(down_project, 0), 0, 4)
     C2.step("end")
+    sums.wait(3)
+    sums.send(4)
     run(functools.partial(up_project, 1), 0, 8)
+    sums.wait(4)
+    sums.send(5)
     run(functools.partial(down_project, 1), 0, 4)
+    sums.wait(5)
 
     pieces = []
     for b in range(images):
@@ -662,19 +675,35 @@
     pooled_all[pl.ds(pl.multiple_of(me_place * 16, 16), 16)] = jnp.concatenate(pieces, axis=0).astype(jnp.bfloat16)
     for stage in range(4):
         pools.send(stage)
-        sums.send(stage + 2)
-        sums.wait(stage + 2)
         pools.wait(stage)
     pooled_f32[...] = pooled_all[...].astype(jnp.float32)
+    load_proj.wait()
+    lanes = me // 16
+    shared = jnp.zeros((128, 256), jnp.float32)
     for b in range(2):
+        content = jnp.zeros((128, 256), jnp.float32)
         for n in range(8):
-            rows = pooled_f32[pl.ds(b * 8 + n, 128, stride=16), :]
-            pooled_out[128 * b : 128 * b + 128, 128 * n : 128 * n + 128] = rows.astype(jnp.bfloat16)
+            rows = pooled_f32[pl.ds(b * 8 + n, 128, stride=16), :].astype(jnp.bfloat16)
+            content += jnp.dot(rows, proj[128 * n : 128 * n + 128], preferred_element_type=jnp.float32)
+        scale = lax.rsqrt(jnp.mean(content * content, axis=-1, keepdims=True) + epsilon)
+        unit = content * scale
+        grad_unit = LOOK_IMG * unit - total_sums[:, 256 * b : 256 * b + 256]
+        inner = jnp.mean(grad_unit * unit, axis=-1, keepdims=True)
+        grad = scale * (grad_unit - unit * inner)
+        at = pl.ds(128 * b, 128)
+        unit_high[at], unit_low[at] = two_parts(unit)
+        grads[at] = grad
+        rows = pooled_f32[pl.ds(b * 8 + lanes, 128, stride=16), :].astype(jnp.bfloat16)
+        for piece in two_parts(grad):
+            shared += lax.dot_general(rows, piece, (((0,), (0,)), ((), ())), preferred_element_type=jnp.float32)
+        content_grad[b : b + 1] = grads[pl.ds(me_place + 128 * b, 1)]
+    columns[...] = shared
+    proj_grad[...] = columns[pl.ds(pl.multiple_of(lax.rem(me, 16) * 8, 8), 8)]
     for weight in (A1, A2, B, C1, C2, D):
         weight.finish()
 
 
-def encode(hidden, gains, lookups, own, table):
+def encode(hidden, gains, lookups, w_proj, own, table):
     width = hidden.shape[2]
     rows = 2 * PAD
     sizes = [(3, width, width // 2)] * 2 + [(width, width)] + [(width, 2 * width)] * 2
@@ -685,13 +714,22 @@
     return pl.pallas_call(
         encoder,
         out_shape=(
-            jax.ShapeDtypeStruct((256, width), bf16),
-            jax.ShapeDtypeStruct((128, 512), f32),
+            jax.ShapeDtypeStruct((256, 256), bf16),
+            jax.ShapeDtypeStruct((256, 256), bf16),
             jax.ShapeDtypeStruct((8, 128), jnp.int32),
+            jax.ShapeDtypeStruct((2, 256), f32),
+            jax.ShapeDtypeStruct((8, 256), f32),
         ),
-        in_specs=[vmem] * 7 + [anywhere] * 5,
-        out_specs=(vmem,) * 3,
-        scratch_shapes=[pltpu.VMEM(s, bf16) for s in sizes]
+        in_specs=[vmem] * 6 + [anywhere] * 7,
+        out_specs=(vmem,) * 5,
+        scratch_shapes=[
+            pltpu.VMEM(hidden.shape, bf16),
+            pltpu.VMEM(w_proj.shape, bf16),
+            pltpu.VMEM((128, 512), f32),
+            pltpu.VMEM((256, 256), f32),
+            pltpu.VMEM((128, 256), f32),
+        ]
+        + [pltpu.VMEM(s, bf16) for s in sizes]
         + [
             pltpu.VMEM((rows, width), bf16),
             pltpu.VMEM((rows, width), bf16),
@@ -712,40 +750,22 @@
             pltpu.SemaphoreType.DMA((SPREAD_SEMS,)),
             pltpu.SemaphoreType.DMA((SPREAD_SEMS,)),
             pltpu.SemaphoreType.DMA((SUMS_SEMS,)),
-            pltpu.SemaphoreType.DMA,
+            pltpu.SemaphoreType.DMA((3,)),
         ],
         compiler_params=pltpu.CompilerParams(
             collective_id=0, has_side_effects=True, vmem_limit_bytes=58 * 1024 * 1024
         ),
         name="encoder",
-    )(hidden, *gains, *lookups, *own, table)
-
-
-def align(pooled, w_proj, sums, codes, table, accum, table_new, accum_new, content_grad, proj_grad, unit, grads, columns):
+    )(*gains, *lookups, hidden, w_proj, *own, table)
+
+
+def align(unit_high, unit_low, codes, content, shared, table, accum, table_new, accum_new, content_grad, proj_grad):
     step = pl.program_id(0)
 
     @pl.when(step == 0)
     def _():
-        y, x, z, c = here()
-        me = ((y * 4 + x) * 4 + z) * 2 + c
-        place = ((c * 4 + z) * 4 + x) * 4 + y
-        content = jnp.dot(pooled[...], w_proj[...], preferred_element_type=jnp.float32)
-        scale = lax.rsqrt(jnp.mean(content * content, axis=-1, keepdims=True) + epsilon)
-        units = content * scale
-        unit[...] = units
-        both = jnp.concatenate([sums[:, 0:256], sums[:, 256:512]], axis=0)
-        grad_unit = LOOK_IMG * units - both
-        inner = jnp.mean(grad_unit * units, axis=-1, keepdims=True)
-        grads[...] = scale * (grad_unit - units * inner)
-        content_grad[0:1] = grads[pl.ds(place, 1)]
-        content_grad[1:2] = grads[pl.ds(place + 128, 1)]
-        lanes = pl.ds(pl.multiple_of(me // 16 * 128, 128), 128)
-        high, low = two_parts(grads[...])
-        turned = lambda right: lax.dot_general(
-            pooled[:, lanes], right, (((0,), (0,)), ((), ())), preferred_element_type=jnp.float32
-        )
-        columns[...] = turned(high) + turned(low)
-        proj_grad[...] = columns[pl.ds(pl.multiple_of(lax.rem(me, 16) * 8, 8), 8)]
+        content_grad[...] = content[...]
+        proj_grad[...] = shared[...]
 
     rows = table.shape[0]
     base = step * rows
@@ -755,15 +775,16 @@
     ]
     hits = jnp.concatenate(hits, axis=1).astype(jnp.bfloat16)
     named = jnp.dot(hits, jnp.ones((256, 128), jnp.bfloat16), preferred_element_type=jnp.float32)[:, 0:1]
-    grad_rows = named * table[...] - split_dot(hits, unit[...])
+    dot = lambda right: jnp.dot(hits, right[...], preferred_element_type=jnp.float32)
+    grad_rows = named * table[...] - (dot(unit_high) + dot(unit_low))
     fresh = accum[...] + grad_rows * grad_rows
     accum_new[...] = fresh
     table_new[...] = table[...] - learn_rate * grad_rows / jnp.sqrt(fresh)
 
 
-def finish(pooled, w_proj, sums, codes, table, accum):
+def finish(small, table, accum):
     n, width = table.shape
-    rows = 512
+    rows = 1024
     whole = lambda a: pl.BlockSpec(a.shape, lambda i: (0, 0))
     tiles = pl.BlockSpec((rows, width), lambda i: (i, 0))
     f32 = jnp.float32
@@ -776,17 +797,16 @@
             jax.ShapeDtypeStruct((2, 256), f32),
             jax.ShapeDtypeStruct((8, 256), f32),
         ),
-        in_specs=[whole(pooled), whole(w_proj), whole(sums), whole(codes), tiles, tiles],
+        in_specs=[whole(a) for a in small] + [tiles, tiles],
         out_specs=(
             tiles,
             tiles,
             pl.BlockSpec((2, 256), lambda i: (0, 0)),
             pl.BlockSpec((8, 256), lambda i: (0, 0)),
         ),
-        scratch_shapes=[pltpu.VMEM((256, 256), f32), pltpu.VMEM((256, 256), f32), pltpu.VMEM((128, 256), f32)],
         compiler_params=pltpu.CompilerParams(dimension_semantics=("arbitrary",)),
         name="align",
-    )(pooled, w_proj, sums, codes, table, accum)
+    )(*small, table, accum)
 
 
 def on_device(
@@ -805,14 +825,15 @@
     lookup_table,
     lookup_row,
 ):
-    pooled, sums, codes = encode(
+    small = encode(
         jnp.swapaxes(hidden, 0, 1),
         (ln1_gain[None, :], ln2_gain[None, :], post_gain[None, :]),
         (lookup_table.reshape(1, -1), lookup_row[None, :], place[None, :]),
+        w_proj,
         (w_qkv, w_out, w_up, w_down),
         table[0],
     )
-    table_new, accum_new, content_grad, proj_grad = finish(pooled, w_proj, sums, codes, table[0], accum[0])
+    table_new, accum_new, content_grad, proj_grad = finish(small, table[0], accum[0])
     return (table_new[None], accum_new[None], content_grad, proj_grad)
 
 

time: 115 us -> 110 us (0.957)
  Pallas kernels: 114 us -> 110 us
    pallas_call x1, Pallas kernels: 107 us -> 105 us  [encode(): pl.pallas_call(encoder, out_shape=(jax.ShapeDtypeStruct((256, 256), bf16)...]
    pallas_call x1, Pallas kernels: 6.83 us -> 5.12 us  [finish(): pl.pallas_call(align, grid=(n // rows,), out_shape=(jax.ShapeDtypeStruct(...]
where the time goes in v4:
time: 110 us
  Pallas kernels  110 us (100%)
    pallas_call x1, Pallas kernels, encode(): pl.pallas_call(encoder, out_shape=(jax.ShapeDtypeStruct((256, 256), bf16)...  105 us
    pallas_call x1, Pallas kernels, finish(): pl.pallas_call(align, grid=(n // rows,), out_shape=(jax.ShapeDtypeStruct(...  5.12 us

profile of v4, /device:TPU:1, one launch (start us, length us, event | category | flops | bytes accessed | tf_op | source)
XLA Modules:
  0.0 110.3 jit_solution(9858822549323396189)
XLA Ops:
  0.6 104.5 %encoder.1 = (bf16[256,256]{1,0:T(8,128)(2,1)}, bf16[256,256]{1,0:T(8,128)(2,1)}, s32[8,128]{1,0:T(8,128)}, f32[2,256]{1,0:T(2,128)}, f32[8,256]{1,0:T(8,128)}) custom-call(f32[1,1024]{1,0:T(1,128)} %bitcast.15, f32[1,1024]{1,0:T(1,128)} %bitcast.16, f32[1,1024]{1,0:T(1,128)} %bitcast.17, s32[1,128]{1,0:T(1,128)} %bitcast.18, s32[1,128]{1,0:T(1,128)} %bitcast.19, ...), custom_call_target="tpu_custom_call" | custom-call | tf_op jit(solution)/shard_map/encoder/pallas_call | solution.py:714
  105.2 5.1 %align.1 = (f32[2048,256]{1,0:T(8,128)}, f32[2048,256]{1,0:T(8,128)}, f32[2,256]{1,0:T(2,128)}, f32[8,256]{1,0:T(8,128)}) custom-call(bf16[256,256]{1,0:T(8,128)(2,1)} %get-tuple-element.13.unit_high, bf16[256,256]{1,0:T(8,128)(2,1)} %get-tuple-element.14.unit_low, s32[8,128]{1,0:T(8,128)} %get-tuple-element.15.codes, f32[2,256]{1,0:T(2,128)} %get-tuple-element.16.content, ...), custom_call_target="tpu_custom_call" | custom-call | tf_op jit(solution)/shard_map/align/pallas_call | solution.py:791
